TPU v7x, 128 devices: a whole 4x4x4 slice. The times are simulated.
128 devices in a mesh: slab: 16 (over y, z), brick: 8 (over x, core).
Axes of the slice: x: 4, y: 4, z: 4, core: 2. Of those that a mesh axis runs over, the one named last changes fastest.
Arguments:
- positions: float32 [8192, 3, 128], P(('slab', 'brick')), may hold values from -6 to 6
- velocities: float32 [8192, 3, 128], P(('slab', 'brick')), may hold values from -6 to 6
- radii: float32 [8192, 128], P(('slab', 'brick')), may hold values from 0.6 to 1.2
- cell_of: int32 [8192, 128], P(('slab', 'brick')), may hold values from 0 to 65535
- block_route: int32 [8192, 1], P(('slab', 'brick')), may hold values from 0 to 23; in each aligned block of 64 rows (0 to 63, 64 to 127, ...) at most 6 rows name the same one
- ghost_list: int32 [2048], P(('slab', 'brick')), may hold values from 0 to 63
- tile_home: int32 [16384], P(('slab', 'brick')), may hold values from 0 to 63
- tile_partner: int32 [16384], P(('slab', 'brick')), may hold values from 0 to 95
- fluid: float32 [3, 64, 256, 512], P(None, 'slab', 'brick'), may hold values from -6 to 6
Outputs:
- velocity_next: float32 [8192, 3, 128], P(('slab', 'brick'))
- fluid_next: float32 [3, 64, 256, 512], P(None, 'slab', 'brick')
Inputs may be any that keep to these rules, and one draw needn't show every extreme that they name: `block_route`: within the blocks of one device no code appears more than 6 times, and some device's blocks reach 6 for some code.
All inputs are finite; a program needn't handle non-finite values.
Results may differ from a plain program's by a relative error of at most 0.00013.
Values sent between devices are 32-bit elements; how exact they have to be, the bound alone decides.
A program may use at most 64 MiB of HBM per device.

v0:
```python
import math

import jax
import jax.numpy as jnp
from jax import lax
from jax.sharding import PartitionSpec as P

stiffness = 0.01
damping = 0.005
viscosity = 0.1
coupling = 0.5
relaxation = 0.5
highest = lax.Precision.HIGHEST


def padded_2(x, sides, width):
    for axis, dim in sides:
        count, length = (lax.axis_size(axis), x.shape[dim])
        up = [(i, (i + 1) % count) for i in range(count)]
        down = [(j, i) for i, j in up]
        last = lax.slice_in_dim(x, length - width, length, axis=dim)
        first = lax.slice_in_dim(x, 0, width, axis=dim)
        before = lax.ppermute(last, axis, up)
        after = lax.ppermute(first, axis, down)
        x = jnp.concatenate([before, x, after], axis=dim)
    return x


def first_dims(left, right):
    return lax.dot_general(left, right, (((0,), (0,)), ((), ())), precision=highest)


def tile_forces(home_block, partner):
    here_pos = home_block[:, 0:3]
    there_pos = partner[:, 0:3]
    here_vel = home_block[:, 3:6]
    there_vel = partner[:, 3:6]
    offsets = here_pos[:, :, :, None] - there_pos[:, :, None, :]
    squared = jnp.sum(offsets * offsets, axis=1)
    contact = home_block[:, 6, :, None] + partner[:, 6, None, :]
    weight = jnp.maximum(contact * contact - squared, 0.0)
    weight_sum = jnp.sum(weight, axis=2)
    spring = jnp.sum(weight[:, None] * offsets, axis=3)
    friction = (
        jnp.einsum("bij,bcj->bci", weight, there_vel, precision=highest)
        - here_vel * weight_sum[:, None]
    )
    return stiffness * spring + damping * friction


def contact_forces(candidates, homes, partners, nblocks):
    count, rows, width = candidates.shape
    flat_cand = candidates.reshape(count, rows * width)
    group = math.gcd(homes.shape[0], 16)
    home_groups = homes.reshape(-1, group)
    partner_groups = partners.reshape(-1, group)
    labels = jnp.arange(count, dtype=jnp.int32)

    def advance_tiles(accumulated, indices):
        home_ids, partner_ids = indices
        home_hot = (home_ids[:, None] == labels[None, :]).astype(jnp.float32)
        partner_hot = (partner_ids[:, None] == labels[None, :]).astype(jnp.float32)
        home_block = jnp.dot(home_hot, flat_cand, precision=highest).reshape(group, rows, width)
        partner = jnp.dot(partner_hot, flat_cand, precision=highest).reshape(group, rows, width)
        terms = tile_forces(home_block, partner).reshape(group, 3 * width)
        added = first_dims(home_hot[:, :nblocks], terms)
        return (accumulated + added, None)

    start = jnp.zeros((nblocks, 3 * width), jnp.float32)
    result, _ = lax.scan(advance_tiles, start, (home_groups, partner_groups))
    return result.reshape(nblocks, 3, width)


def hot_tables(piece, columns, depth):
    cell_index = piece[:, 4].reshape(-1).astype(jnp.int32)
    column = cell_index // depth
    level = cell_index % depth
    col_hot = (column[:, None] == jnp.arange(columns, dtype=jnp.int32)[None, :]).astype(jnp.float32)
    z_hot = (level[:, None] == jnp.arange(depth, dtype=jnp.int32)[None, :]).astype(jnp.float32)
    return (col_hot, z_hot)


def advance_fluid(arrived, fluid):
    slots, _, width = arrived.shape
    columns = fluid.shape[1] * fluid.shape[2]
    depth = fluid.shape[3]
    group = math.gcd(slots, 8)
    grouped = arrived.reshape(slots // group, group, 5, width)

    def deposit(total, piece):
        col_hot, z_hot = hot_tables(piece, columns, depth)
        radius_in = piece[:, 0].reshape(-1)
        speeds = jnp.transpose(piece[:, 1:4], (0, 2, 1)).reshape(-1, 3)
        masses = radius_in * radius_in * radius_in
        loads = jnp.concatenate([masses[:, None], masses[:, None] * speeds], axis=1)
        left = (loads[:, :, None] * col_hot[:, None, :]).reshape(-1, 4 * columns)
        return (total + first_dims(left, z_hot), None)

    start = jnp.zeros((4 * columns, depth), jnp.float32)
    deposited, _ = lax.scan(deposit, start, grouped)
    deposited = deposited.reshape(4, fluid.shape[1], fluid.shape[2], depth)
    volume = deposited[0]
    momentum = deposited[1:4]
    padded = padded_2(fluid, (("slab", 1), ("brick", 2)), 1)
    padded = jnp.pad(padded, ((0, 0), (0, 0), (0, 0), (1, 1)))
    center = padded[:, 1:-1, 1:-1, 1:-1]
    total = padded[:, 2:, 1:-1, 1:-1] + padded[:, :-2, 1:-1, 1:-1]
    total = total + padded[:, 1:-1, 2:, 1:-1] + padded[:, 1:-1, :-2, 1:-1]
    total = total + padded[:, 1:-1, 1:-1, 2:] + padded[:, 1:-1, 1:-1, :-2]
    laplacian = total - 6.0 * center
    fluid_next = fluid + viscosity * laplacian + coupling * (momentum - volume * fluid)
    flat_fluid = fluid_next.reshape(3 * columns, depth)

    def sample(carry, piece):
        col_hot, z_hot = hot_tables(piece, columns, depth)
        along = lax.dot_general(z_hot, flat_fluid, (((1,), (1,)), ((), ())), precision=highest)
        picked = jnp.sum(along.reshape(-1, 3, columns) * col_hot[:, None, :], axis=2)
        return (carry, jnp.transpose(picked.reshape(group, width, 3), (0, 2, 1)))

    _, sampled = lax.scan(sample, 0, grouped)
    return (fluid_next, sampled.reshape(slots, 3, width))


def on_device(
    positions, velocities, radii, cell_of, block_route, ghost_list, tile_home, tile_partner, fluid
):
    nblocks, _, width = positions.shape
    ghost_count = ghost_list.shape[0] // 4
    owned = jnp.concatenate([positions, velocities, radii[:, None, :]], axis=1)
    ghost_sets = owned[ghost_list].reshape(2, 2, ghost_count, 7, width)
    widened = padded_2(ghost_sets, (("slab", 0), ("brick", 1)), 1)
    candidates = jnp.concatenate(
        [
            owned,
            widened[0, 1:3].reshape(-1, 7, width),
            widened[3, 1:3].reshape(-1, 7, width),
            widened[1:3, 0].reshape(-1, 7, width),
            widened[1:3, 3].reshape(-1, 7, width),
        ],
        axis=0,
    )
    forces = contact_forces(candidates, tile_home, tile_partner, nblocks)
    masses = radii * radii * radii
    updated = velocities + forces / masses[:, None, :]
    payload = jnp.concatenate(
        [radii[:, None, :], updated, cell_of.astype(jnp.float32)[:, None, :]], axis=1
    )
    flat_payload = payload.reshape(nblocks, 5 * width)
    nbrick = lax.axis_size("brick")
    route_code = block_route[:, 0]
    offset_code = route_code // nbrick
    target_brick = route_code % nbrick
    code_count = 3 * nbrick
    capacity = max(2, (2 * nblocks + code_count - 1) // code_count)
    slot_total = code_count * capacity
    matches = (route_code[:, None] == jnp.arange(code_count, dtype=jnp.int32)[None, :]).astype(
        jnp.int32
    )
    position = jnp.sum((jnp.cumsum(matches, axis=0) - matches) * matches, axis=1)
    slot_labels = jnp.arange(slot_total, dtype=jnp.int32)
    slot_index = (offset_code * nbrick + target_brick) * capacity + position
    slot_hot = (slot_index[:, None] == slot_labels[None, :]).astype(jnp.float32)
    outgoing = first_dims(slot_hot, flat_payload)
    outgoing = outgoing.reshape(1, 3, nbrick, capacity, 5, width)
    spread = padded_2(outgoing, (("slab", 0),), 1)
    bound_here = jnp.stack([spread[0, 2], spread[1, 1], spread[2, 0]], axis=0)
    arrived = lax.all_to_all(bound_here, "brick", split_axis=1, concat_axis=1, tiled=True).reshape(
        -1, 5, width
    )
    fluid_next, sampled = advance_fluid(arrived, fluid)
    answers = sampled.reshape(3, nbrick, capacity, 3, width)
    answers = lax.all_to_all(answers, "brick", split_axis=1, concat_axis=1, tiled=True)
    spread_back = padded_2(answers[None], (("slab", 0),), 1)
    returned = jnp.stack([spread_back[0, 2], spread_back[1, 1], spread_back[2, 0]], axis=0)
    returned = returned.reshape(-1, 3, width)
    picked = jnp.dot(slot_hot, returned.reshape(slot_total, 3 * width), precision=highest).reshape(
        nblocks, 3, width
    )
    velocity_next = updated + relaxation * (picked - updated)
    return (velocity_next, fluid_next)


def solution(mesh):
    placed = (
        P(("slab", "brick"), None, None),
        P(("slab", "brick"), None, None),
        P(("slab", "brick"), None),
        P(("slab", "brick"), None),
        P(("slab", "brick"), None),
        P(("slab", "brick")),
        P(("slab", "brick")),
        P(("slab", "brick")),
        P(None, "slab", "brick", None),
    )
    return jax.shard_map(
        on_device,
        mesh=mesh,
        in_specs=placed,
        out_specs=(P(("slab", "brick"), None, None), P(None, "slab", "brick", None)),
        check_vma=False,
    )
```

profile of v0, /device:TPU:1, one launch (start us, length us, event | category | flops | bytes accessed | tf_op | source)
XLA Modules:
  0.0 353.6 jit_solution(5435342222654728379)
XLA Ops:
  7.3 4.7 %collective-permute-start.1 = (f32[1,2,4,7,128]{4,3,2,0,1:T(8,128)S(1)}, f32[1,2,4,7,128]{4,3,2,0,1:T(8,128)S(1)}, u32[]{:S(2)}, u32[]{:S(2)}) collective-permute-start(f32[1,2,4,7,128]{4,3,2,0,1:T(8,128)S(1)} %bitcast.254), channel_id=1, source_target_pairs={{8,0},{16,8},{24,16},{32,24},{40,32},{48,40},{56,48},{64,56},{72,6... | collective-permute-start | bytes 86024 | tf_op jit(solution)/shard_map/ppermute | solution.py:24
  13.1 4.8 %collective-permute-start.6 = (f32[3,1,32,512]{3,2,1,0:T(8,128)S(1)}, f32[3,1,32,512]{3,2,1,0:T(8,128)S(1)}, u32[]{:S(2)}, u32[]{:S(2)}) collective-permute-start(f32[3,1,32,512]{3,2,1,0:T(8,128)S(1)} %get-tuple-element.257), channel_id=1, source_target_pairs={{8,0},{16,8},{24,16},{32,24},{40,32},{48,40},{56,48},{64,56},{72,6... | collective-permute-start | bytes 589832 | tf_op jit(solution)/shard_map/ppermute | solution.py:24
  24.9 50.4 %while.39 = (s32[]{:T(128)}, f32[64,384]{1,0:T(8,128)S(1)}, s32[8,16]{1,0:T(8,128)S(1)}, f32[96,896]{1,0:T(8,128)S(1)}, s32[8,16]{1,0:T(8,128)S(1)}, /*index=5*/s32[]{:T(128)}, s32[]{:T(128)}) while((s32[]{:T(128)}, f32[64,384]{1,0:T(8,128)S(1)}, s32[8,16]{1,0:T(8,128)S(1)}, f32[96,896]{1,0:T(8,128)S(1)}, ...), condition=%wide.region_4.5_spmd.clone.clone, body=%wide.region_0.4_spmd.clone.clone.sunk | while | flops 53029376 | bytes 6909467 | solution.py:70
  77.5 8.4 %collective-permute-done.5 = f32[1,3,8,6,5,128]{5,2,4,3,1,0:T(8,128)S(1)} collective-permute-done((f32[1,3,8,6,5,128]{5,2,4,3,1,0:T(8,128)S(1)}, f32[1,3,8,6,5,128]{5,2,4,3,1,0:T(8,128)S(1)}, u32[]{:S(2)}, u32[]{:S(2)}) %collective-permute-start.5) | collective-permute-done | bytes 368672 | tf_op jit(solution)/shard_map/ppermute | solution.py:24
  96.4 6.7 %collective-permute-done.8 = f32[3,6,1,512]{3,2,1,0:T(1,128)S(1)} collective-permute-done((f32[3,6,1,512]{3,2,1,0:T(1,128)S(1)}, f32[3,6,1,512]{3,2,1,0:T(1,128)S(1)}, u32[]{:S(2)}, u32[]{:S(2)}) %collective-permute-start.8) | collective-permute-done | bytes 36896 | tf_op jit(solution)/shard_map/ppermute | solution.py:24
  105.3 172.9 %while.38 = (s32[]{:T(128)}, f32[512,512]{1,0:T(8,128)}, f32[18,8,5,128]{3,1,0,2:T(8,128)S(1)}, s32[]{:T(128)}, s32[]{:T(128)}) while((s32[]{:T(128)}, f32[512,512]{1,0:T(8,128)}, f32[18,8,5,128]{3,1,0,2:T(8,128)S(1)}, s32[]{:T(128)}, s32[]{:T(128)}) %tuple.104), condition=%wide.region_8.9_spmd.clone, body=%wide.region_7.8_spmd.clone.sunk | while | flops 3223099392 | bytes 10516611 | solution.py:100
  118.8 4.5 %fusion.93 = f32[512,512]{1,0:T(8,128)} fusion(f32[128,8,4,128]{3,2,1,0:T(4,128)S(1)} %bitcast.229, f32[512,512]{1,0:T(8,128)} %get-tuple-element.381, s32[1024]{0:T(1024)S(1)} %get-tuple-element.344, pred[]{:T(512)S(6)} %compare.50), kind=kOutput, calls=%fused_computation.25.clone.1 | convolution fusion | flops 3222274048 | bytes 4198401 | tf_op jit(solution)/shard_map/while/body/eval_jaxpr/dot_general | solution.py:30
  128.5 4.5 %fusion.93 = f32[512,512]{1,0:T(8,128)} fusion(f32[128,8,4,128]{3,2,1,0:T(4,128)S(1)} %bitcast.229, f32[512,512]{1,0:T(8,128)} %get-tuple-element.381, s32[1024]{0:T(1024)S(1)} %get-tuple-element.344, pred[]{:T(512)S(6)} %compare.50), kind=kOutput, calls=%fused_computation.25.clone.1 | convolution fusion | flops 3222274048 | bytes 4198401 | tf_op jit(solution)/shard_map/while/body/eval_jaxpr/dot_general | solution.py:30
  138.2 4.5 %fusion.93 = f32[512,512]{1,0:T(8,128)} fusion(f32[128,8,4,128]{3,2,1,0:T(4,128)S(1)} %bitcast.229, f32[512,512]{1,0:T(8,128)} %get-tuple-element.381, s32[1024]{0:T(1024)S(1)} %get-tuple-element.344, pred[]{:T(512)S(6)} %compare.50), kind=kOutput, calls=%fused_computation.25.clone.1 | convolution fusion | flops 3222274048 | bytes 4198401 | tf_op jit(solution)/shard_map/while/body/eval_jaxpr/dot_general | solution.py:30
  147.9 4.5 %fusion.93 = f32[512,512]{1,0:T(8,128)} fusion(f32[128,8,4,128]{3,2,1,0:T(4,128)S(1)} %bitcast.229, f32[512,512]{1,0:T(8,128)} %get-tuple-element.381, s32[1024]{0:T(1024)S(1)} %get-tuple-element.344, pred[]{:T(512)S(6)} %compare.50), kind=kOutput, calls=%fused_computation.25.clone.1 | convolution fusion | flops 3222274048 | bytes 4198401 | tf_op jit(solution)/shard_map/while/body/eval_jaxpr/dot_general | solution.py:30
  157.5 4.5 %fusion.93 = f32[512,512]{1,0:T(8,128)} fusion(f32[128,8,4,128]{3,2,1,0:T(4,128)S(1)} %bitcast.229, f32[512,512]{1,0:T(8,128)} %get-tuple-element.381, s32[1024]{0:T(1024)S(1)} %get-tuple-element.344, pred[]{:T(512)S(6)} %compare.50), kind=kOutput, calls=%fused_computation.25.clone.1 | convolution fusion | flops 3222274048 | bytes 4198401 | tf_op jit(solution)/shard_map/while/body/eval_jaxpr/dot_general | solution.py:30
  167.2 4.5 %fusion.93 = f32[512,512]{1,0:T(8,128)} fusion(f32[128,8,4,128]{3,2,1,0:T(4,128)S(1)} %bitcast.229, f32[512,512]{1,0:T(8,128)} %get-tuple-element.381, s32[1024]{0:T(1024)S(1)} %get-tuple-element.344, pred[]{:T(512)S(6)} %compare.50), kind=kOutput, calls=%fused_computation.25.clone.1 | convolution fusion | flops 3222274048 | bytes 4198401 | tf_op jit(solution)/shard_map/while/body/eval_jaxpr/dot_general | solution.py:30
  176.9 4.5 %fusion.93 = f32[512,512]{1,0:T(8,128)} fusion(f32[128,8,4,128]{3,2,1,0:T(4,128)S(1)} %bitcast.229, f32[512,512]{1,0:T(8,128)} %get-tuple-element.381, s32[1024]{0:T(1024)S(1)} %get-tuple-element.344, pred[]{:T(512)S(6)} %compare.50), kind=kOutput, calls=%fused_computation.25.clone.1 | convolution fusion | flops 3222274048 | bytes 4198401 | tf_op jit(solution)/shard_map/while/body/eval_jaxpr/dot_general | solution.py:30
  186.5 4.5 %fusion.93 = f32[512,512]{1,0:T(8,128)} fusion(f32[128,8,4,128]{3,2,1,0:T(4,128)S(1)} %bitcast.229, f32[512,512]{1,0:T(8,128)} %get-tuple-element.381, s32[1024]{0:T(1024)S(1)} %get-tuple-element.344, pred[]{:T(512)S(6)} %compare.50), kind=kOutput, calls=%fused_computation.25.clone.1 | convolution fusion | flops 3222274048 | bytes 4198401 | tf_op jit(solution)/shard_map/while/body/eval_jaxpr/dot_general | solution.py:30
  205.9 4.5 %fusion.93 = f32[512,512]{1,0:T(8,128)} fusion(f32[128,8,4,128]{3,2,1,0:T(4,128)S(1)} %bitcast.229, f32[512,512]{1,0:T(8,128)} %get-tuple-element.381, s32[1024]{0:T(1024)S(1)} %get-tuple-element.344, pred[]{:T(512)S(6)} %compare.50), kind=kOutput, calls=%fused_computation.25.clone.1 | convolution fusion | flops 3222274048 | bytes 4198401 | tf_op jit(solution)/shard_map/while/body/eval_jaxpr/dot_general | solution.py:30
  215.6 4.5 %fusion.93 = f32[512,512]{1,0:T(8,128)} fusion(f32[128,8,4,128]{3,2,1,0:T(4,128)S(1)} %bitcast.229, f32[512,512]{1,0:T(8,128)} %get-tuple-element.381, s32[1024]{0:T(1024)S(1)} %get-tuple-element.344, pred[]{:T(512)S(6)} %compare.50), kind=kOutput, calls=%fused_computation.25.clone.1 | convolution fusion | flops 3222274048 | bytes 4198401 | tf_op jit(solution)/shard_map/while/body/eval_jaxpr/dot_general | solution.py:30
  225.2 4.5 %fusion.93 = f32[512,512]{1,0:T(8,128)} fusion(f32[128,8,4,128]{3,2,1,0:T(4,128)S(1)} %bitcast.229, f32[512,512]{1,0:T(8,128)} %get-tuple-element.381, s32[1024]{0:T(1024)S(1)} %get-tuple-element.344, pred[]{:T(512)S(6)} %compare.50), kind=kOutput, calls=%fused_computation.25.clone.1 | convolution fusion | flops 3222274048 | bytes 4198401 | tf_op jit(solution)/shard_map/while/body/eval_jaxpr/dot_general | solution.py:30
  234.9 4.5 %fusion.93 = f32[512,512]{1,0:T(8,128)} fusion(f32[128,8,4,128]{3,2,1,0:T(4,128)S(1)} %bitcast.229, f32[512,512]{1,0:T(8,128)} %get-tuple-element.381, s32[1024]{0:T(1024)S(1)} %get-tuple-element.344, pred[]{:T(512)S(6)} %compare.50), kind=kOutput, calls=%fused_computation.25.clone.1 | convolution fusion | flops 3222274048 | bytes 4198401 | tf_op jit(solution)/shard_map/while/body/eval_jaxpr/dot_general | solution.py:30
  244.6 4.5 %fusion.93 = f32[512,512]{1,0:T(8,128)} fusion(f32[128,8,4,128]{3,2,1,0:T(4,128)S(1)} %bitcast.229, f32[512,512]{1,0:T(8,128)} %get-tuple-element.381, s32[1024]{0:T(1024)S(1)} %get-tuple-element.344, pred[]{:T(512)S(6)} %compare.50), kind=kOutput, calls=%fused_computation.25.clone.1 | convolution fusion | flops 3222274048 | bytes 4198401 | tf_op jit(solution)/shard_map/while/body/eval_jaxpr/dot_general | solution.py:30
  263.9 4.5 %fusion.93 = f32[512,512]{1,0:T(8,128)} fusion(f32[128,8,4,128]{3,2,1,0:T(4,128)S(1)} %bitcast.229, f32[512,512]{1,0:T(8,128)} %get-tuple-element.381, s32[1024]{0:T(1024)S(1)} %get-tuple-element.344, pred[]{:T(512)S(6)} %compare.50), kind=kOutput, calls=%fused_computation.25.clone.1 | convolution fusion | flops 3222274048 | bytes 4198401 | tf_op jit(solution)/shard_map/while/body/eval_jaxpr/dot_general | solution.py:30
  273.6 4.5 %fusion.93 = f32[512,512]{1,0:T(8,128)} fusion(f32[128,8,4,128]{3,2,1,0:T(4,128)S(1)} %bitcast.229, f32[512,512]{1,0:T(8,128)} %get-tuple-element.381, s32[1024]{0:T(1024)S(1)} %get-tuple-element.344, pred[]{:T(512)S(6)} %compare.50), kind=kOutput, calls=%fused_computation.25.clone.1 | convolution fusion | flops 3222274048 | bytes 4198401 | tf_op jit(solution)/shard_map/while/body/eval_jaxpr/dot_general | solution.py:30
  282.6 46.5 %while.37 = (s32[]{:T(128)}, f32[18,8,3,128]{3,1,0,2:T(8,128)}, f32[18,8,5,128]{3,1,0,2:T(8,128)S(1)}, f32[384,512]{1,0:T(8,128)S(1)}, s32[]{:T(128)}) while((s32[]{:T(128)}, f32[18,8,3,128]{3,1,0,2:T(8,128)}, f32[18,8,5,128]{3,1,0,2:T(8,128)S(1)}, f32[384,512]{1,0:T(8,128)S(1)}, s32[]{:T(128)}) %tuple.111), condition=%wide.region_11.12_spmd, body=%wide.region_9.11_spmd.sunk | while | flops 2417509376 | bytes 5128769 | solution.py:120
  330.4 10.9 %all_to_all.10 = f32[3,8,6,3,128]{4,2,0,3,1:T(8,128)S(1)} all-to-all(f32[3,8,6,3,128]{4,2,0,3,1:T(8,128)S(1)} %copy.102), channel_id=1, replica_groups=mesh['slab'=16,'brick'=8] {'brick'}, dimensions={1} | all-to-all | bytes 442368 | tf_op jit(solution)/shard_map/all_to_all | solution.py:172
  342.9 9.7 %collective-permute-done.10 = f32[1,3,8,6,3,128]{5,3,4,2,1,0:T(8,128)S(1)} collective-permute-done((f32[1,3,8,6,3,128]{5,3,4,2,1,0:T(8,128)S(1)}, f32[1,3,8,6,3,128]{5,3,4,2,1,0:T(8,128)S(1)}, u32[]{:S(2)}, u32[]{:S(2)}) %collective-permute-start.10) | collective-permute-done | bytes 221216 | tf_op jit(solution)/shard_map/ppermute | solution.py:23
  (665 shorter events, 236.1 us)
Async XLA Ops:
  0.6 17.2 %copy-start.10 = (f32[64,128]{1,0:T(8,128)S(1)}, f32[64,128]{1,0:T(8,128)}, u32[]{:S(2)}) copy-start(f32[64,128]{1,0:T(8,128)} %param.17) | copy-start | bytes 98308
  0.6 17.3 %copy-start.13 = (s32[64,128]{1,0:T(8,128)S(1)}, s32[64,128]{1,0:T(8,128)}, u32[]{:S(2)}) copy-start(s32[64,128]{1,0:T(8,128)} %param.18) | copy-start | bytes 98308
  0.7 17.3 %copy-start.14 = (s32[64,1]{0,1:T(1,128)S(1)}, s32[64,1]{0,1:T(1,128)}, u32[]{:S(2)}) copy-start(s32[64,1]{0,1:T(1,128)} %param.19) | copy-start | bytes 772
  0.7 17.7 %copy-start.15 = (s32[128]{0:T(128)S(1)}, s32[128]{0:T(128)}, u32[]{:S(2)}) copy-start(s32[128]{0:T(128)} %param.21) | copy-start | bytes 1540
  0.7 17.8 %copy-start.16 = (s32[128]{0:T(128)S(1)}, s32[128]{0:T(128)}, u32[]{:S(2)}) copy-start(s32[128]{0:T(128)} %param.22) | copy-start | bytes 1540
  4.8 13.8 %collective-permute-start = (f32[1,2,4,7,128]{4,3,2,0,1:T(8,128)S(1)}, f32[1,2,4,7,128]{4,3,2,0,1:T(8,128)S(1)}, u32[]{:S(2)}, u32[]{:S(2)}) collective-permute-start(f32[1,2,4,7,128]{4,3,2,0,1:T(8,128)S(1)} %bitcast.255), channel_id=1, source_target_pairs={{0,8},{8,16},{16,24},{24,32},{32,40},{40,48},{48,56},{56,64},{64,7... | collective-permute-start | bytes 86024 | tf_op jit(solution)/shard_map/ppermute | solution.py:23
  7.3 11.3 %collective-permute-start.1 = (f32[1,2,4,7,128]{4,3,2,0,1:T(8,128)S(1)}, f32[1,2,4,7,128]{4,3,2,0,1:T(8,128)S(1)}, u32[]{:S(2)}, u32[]{:S(2)}) collective-permute-start(f32[1,2,4,7,128]{4,3,2,0,1:T(8,128)S(1)} %bitcast.254), channel_id=1, source_target_pairs={{8,0},{16,8},{24,16},{32,24},{40,32},{48,40},{56,48},{64,56},{72,6... | collective-permute-start | bytes 86024 | tf_op jit(solution)/shard_map/ppermute | solution.py:24
  13.0 64.3 %collective-permute-start.7 = (f32[3,1,32,512]{3,2,1,0:T(8,128)S(1)}, f32[3,1,32,512]{3,2,1,0:T(8,128)S(1)}, u32[]{:S(2)}, u32[]{:S(2)}) collective-permute-start(f32[3,1,32,512]{3,2,1,0:T(8,128)S(1)} %get-tuple-element.258), channel_id=1, source_target_pairs={{0,8},{8,16},{16,24},{24,32},{32,40},{40,48},{48,56},{56,64},{64,7... | collective-permute-start | bytes 589832 | tf_op jit(solution)/shard_map/ppermute | solution.py:23
  13.1 64.4 %collective-permute-start.6 = (f32[3,1,32,512]{3,2,1,0:T(8,128)S(1)}, f32[3,1,32,512]{3,2,1,0:T(8,128)S(1)}, u32[]{:S(2)}, u32[]{:S(2)}) collective-permute-start(f32[3,1,32,512]{3,2,1,0:T(8,128)S(1)} %get-tuple-element.257), channel_id=1, source_target_pairs={{8,0},{16,8},{24,16},{32,24},{40,32},{48,40},{56,48},{64,56},{72,6... | collective-permute-start | bytes 589832 | tf_op jit(solution)/shard_map/ppermute | solution.py:24
  18.6 4.0 %collective-permute-start.2 = (f32[4,1,4,7,128]{4,3,2,0,1:T(8,128)S(1)}, f32[4,1,4,7,128]{4,3,2,0,1:T(8,128)S(1)}, u32[]{:S(2)}, u32[]{:S(2)}) collective-permute-start(f32[4,1,4,7,128]{4,3,2,0,1:T(8,128)S(1)} %get-tuple-element.260), channel_id=1, source_target_pairs={{0,1},{1,2},{2,3},{3,4},{4,5},{5,6},{6,7},{7,0},{8,9},{9,10},{10,1... | collective-permute-start | bytes 172040 | tf_op jit(solution)/shard_map/ppermute | solution.py:23
  21.2 3.7 %collective-permute-start.3 = (f32[4,1,4,7,128]{4,3,2,0,1:T(8,128)S(1)}, f32[4,1,4,7,128]{4,3,2,0,1:T(8,128)S(1)}, u32[]{:S(2)}, u32[]{:S(2)}) collective-permute-start(f32[4,1,4,7,128]{4,3,2,0,1:T(8,128)S(1)} %get-tuple-element.259), channel_id=1, source_target_pairs={{1,0},{2,1},{3,2},{4,3},{5,4},{6,5},{7,6},{0,7},{9,8},{10,9},{11,1... | collective-permute-start | bytes 172040 | tf_op jit(solution)/shard_map/ppermute | solution.py:24
  24.9 50.4 %copy-start.9 = (f32[64,3,128]{2,0,1:T(8,128)S(1)}, f32[64,3,128]{2,0,1:T(8,128)}, u32[]{:S(2)}) copy-start(f32[64,3,128]{2,0,1:T(8,128)} %param.16) | copy-start | bytes 294916
  75.8 10.1 %collective-permute-start.5 = (f32[1,3,8,6,5,128]{5,2,4,3,1,0:T(8,128)S(1)}, f32[1,3,8,6,5,128]{5,2,4,3,1,0:T(8,128)S(1)}, u32[]{:S(2)}, u32[]{:S(2)}) collective-permute-start(f32[1,3,8,6,5,128]{5,2,4,3,1,0:T(8,128)S(1)} %convolution_bitcast_fusion), channel_id=1, source_target_pairs={{8,0},{16,8},{24,16},{32,24},{40,32},{48,40},{56,48},{64,56},{72,6... | collective-permute-start | bytes 1105928 | tf_op jit(solution)/shard_map/ppermute | solution.py:24
  75.9 13.4 %collective-permute-start.4 = (f32[1,3,8,6,5,128]{5,2,4,3,1,0:T(8,128)S(1)}, f32[1,3,8,6,5,128]{5,2,4,3,1,0:T(8,128)S(1)}, u32[]{:S(2)}, u32[]{:S(2)}) collective-permute-start(f32[1,3,8,6,5,128]{5,2,4,3,1,0:T(8,128)S(1)} %convolution_bitcast_fusion), channel_id=1, source_target_pairs={{0,8},{8,16},{16,24},{24,32},{32,40},{40,48},{48,56},{56,64},{64,7... | collective-permute-start | bytes 1105928 | tf_op jit(solution)/shard_map/ppermute | solution.py:23
  77.3 11.9 %copy-start.6 = (f32[3,1,32,512]{3,2,1,0:T(8,128)}, f32[3,1,32,512]{3,2,1,0:T(8,128)S(1)}, u32[]{:S(2)}) copy-start(f32[3,1,32,512]{3,2,1,0:T(8,128)S(1)} %collective-permute-done.7) | copy-start | bytes 589828
  77.5 11.8 %copy-start.8 = (f32[3,1,32,512]{3,2,1,0:T(8,128)}, f32[3,1,32,512]{3,2,1,0:T(8,128)S(1)}, u32[]{:S(2)}) copy-start(f32[3,1,32,512]{3,2,1,0:T(8,128)S(1)} %collective-permute-done.6) | copy-start | bytes 589828
  77.5 27.7 %copy-start.2 = (f32[3,6,32,512]{3,2,1,0:T(8,128)}, f32[3,6,32,512]{3,2,1,0:T(8,128)S(1)}, u32[]{:S(2)}) copy-start(f32[3,6,32,512]{3,2,1,0:T(8,128)S(1)} %constant_dynamic-update-slice_fusion.2) | copy-start | bytes 3538948
  90.2 15.0 %all-to-all-start = ((f32[3,8,6,5,128]{4,2,3,0,1:T(8,128)}), f32[3,8,6,5,128]{4,2,3,0,1:T(8,128)S(1)}, u32[]{:S(2)}, u32[]{:S(2)}) async-start(f32[3,8,6,5,128]{4,2,3,0,1:T(8,128)} %copy.97), calls=%async_computation | async-start | bytes 983040 | tf_op jit(solution)/shard_map/all_to_all | solution.py:167
  94.6 8.4 %collective-permute-start.8 = (f32[3,6,1,512]{3,2,1,0:T(1,128)S(1)}, f32[3,6,1,512]{3,2,1,0:T(1,128)S(1)}, u32[]{:S(2)}, u32[]{:S(2)}) collective-permute-start(f32[3,6,1,512]{3,2,1,0:T(1,128)S(1)} %get-tuple-element.256), channel_id=1, source_target_pairs={{1,0},{2,1},{3,2},{4,3},{5,4},{6,5},{7,6},{0,7},{9,8},{10,9},{11,1... | collective-permute-start | bytes 110600 | tf_op jit(solution)/shard_map/ppermute | solution.py:24
  94.9 8.1 %collective-permute-start.9 = (f32[3,6,1,512]{3,2,1,0:T(1,128)S(1)}, f32[3,6,1,512]{3,2,1,0:T(1,128)S(1)}, u32[]{:S(2)}, u32[]{:S(2)}) collective-permute-start(f32[3,6,1,512]{3,2,1,0:T(1,128)S(1)} %get-tuple-element.255), channel_id=1, source_target_pairs={{0,1},{1,2},{2,3},{3,4},{4,5},{5,6},{6,7},{7,0},{8,9},{9,10},{10,1... | collective-permute-start | bytes 110600 | tf_op jit(solution)/shard_map/ppermute | solution.py:23
  128.5 4.6 %copy-start.5 = (f32[18,8,5,128]{3,1,0,2:T(8,128)S(1)}, f32[18,8,5,128]{3,1,0,2:T(8,128)}, u32[]{:S(2)}) copy-start(f32[18,8,5,128]{3,1,0,2:T(8,128)} %copy-done.4) | copy-start | bytes 1105924 | tf_op jit(solution)/shard_map/while
  329.1 23.6 %copy-start = (f32[384,512]{1,0:T(8,128)}, f32[384,512]{1,0:T(8,128)S(1)}, u32[]{:S(2)}) copy-start(f32[384,512]{1,0:T(8,128)S(1)} %get-tuple-element.405) | copy-start | bytes 2359300
  341.3 11.3 %collective-permute-start.11 = (f32[1,3,8,6,3,128]{5,3,1,4,2,0:T(8,128)S(1)}, f32[1,3,8,6,3,128]{5,3,1,4,2,0:T(8,128)S(1)}, u32[]{:S(2)}, u32[]{:S(2)}) collective-permute-start(f32[1,3,8,6,3,128]{5,3,1,4,2,0:T(8,128)S(1)} %bitcast.235), channel_id=1, source_target_pairs={{8,0},{16,8},{24,16},{32,24},{40,32},{48,40},{56,48},{64,56},{72,6... | collective-permute-start | bytes 663560 | tf_op jit(solution)/shard_map/ppermute | solution.py:24
  341.4 11.2 %collective-permute-start.10 = (f32[1,3,8,6,3,128]{5,3,4,2,1,0:T(8,128)S(1)}, f32[1,3,8,6,3,128]{5,3,4,2,1,0:T(8,128)S(1)}, u32[]{:S(2)}, u32[]{:S(2)}) collective-permute-start(f32[1,3,8,6,3,128]{5,3,4,2,1,0:T(8,128)S(1)} %copy.103), channel_id=1, source_target_pairs={{0,8},{8,16},{16,24},{24,32},{32,40},{40,48},{48,56},{56,64},{64,7... | collective-permute-start | bytes 663560 | tf_op jit(solution)/shard_map/ppermute | solution.py:23
  (40 other events, 100.7 us)
where the time goes:
time: 355 us; the launch traced here: 354 us
  matrix products  132 us (37%)
  other arithmetic  115 us (32%)
  local copies, waits for them, and re-layouts  36.6 us (10%)
  waiting for transfers between devices  31.8 us (9%)
  starting transfers between devices  23.8 us (7%)
  blocking collectives  10.9 us (3%)
    dot_general x27, matrix products, first_dims(): lax.dot_general(left, right, (((0,), (0,)), ((), ())), precision=highest)  83.1 us
    mul x18, other arithmetic, deposit(): left = (loads[:, :, None] * col_hot[:, None, :]).reshape(-1, 4 * columns)  69.8 us
    dot_general x18, matrix products, sample(): lax.dot_general(z_hot, flat_fluid, (((1,), (1,)), ((), ())), precision=hi...  29.7 us
    ppermute x6, waiting for transfers between devices, padded_2(): after = lax.ppermute(first, axis, down)  17.4 us
    reduce_sum x8, other arithmetic, tile_forces(): spring = jnp.sum(weight[:, None] * offsets, axis=3)  14.9 us
    ppermute x6, waiting for transfers between devices, padded_2(): before = lax.ppermute(last, axis, up)  14.4 us
    dot_general x8, matrix products, tile_forces(): jnp.einsum('bij,bcj->bci', weight, there_vel, precision=highest)  13.9 us
    while x90, local copies, waits for them, and re-layouts  12.2 us
  transfers between devices with their start and end apart: 13, of which 6 were waited for; matrix products, arithmetic and copies ran while one was open for 15% of the time, Pallas kernels for 0%

commit v1 on v0

v1 whole, which is shorter than its diff:
```python
import functools

import jax
import jax.numpy as jnp
from jax import lax
from jax.experimental import pallas as pl
from jax.experimental.pallas import tpu as pltpu
from jax.sharding import PartitionSpec as P

stiffness = 0.01
damping = 0.005
viscosity = 0.1
coupling = 0.5
relaxation = 0.5

MESH = pl.DeviceIdType.MESH
F32 = jnp.float32
BF16 = jnp.bfloat16
VMEM = pl.BlockSpec(memory_space=pltpu.VMEM)
SMEM = pl.BlockSpec(memory_space=pltpu.SMEM)

N_SLAB = 16
N_BRICK = 8
NB = 64
BLK = 128
TILES = 128
CAND = 96
CODES = 24
CAP = 6
SEND_ROWS = 32
BACK_ROWS = 24
COLS = 128
DEPTH = 512
CHUNK = 2


def iota(shape, dim, dtype=jnp.int32):
    return lax.broadcasted_iota(jnp.int32, shape, dim).astype(dtype)


def split3(x):
    high = x.astype(BF16)
    rest = x - high.astype(F32)
    middle = rest.astype(BF16)
    low = (rest - middle.astype(F32)).astype(BF16)
    return high, middle, low


def split2(x):
    high = x.astype(BF16)
    return high, (x - high.astype(F32)).astype(BF16)


def params(mib, collective_id=None):
    return pltpu.CompilerParams(
        vmem_limit_bytes=mib << 20,
        collective_id=collective_id,
        has_side_effects=collective_id is not None,
    )


def halo_kernel(
    glist, pos, vel, rad, fluid, ghosts, xlo, xhi, ylo, yhi, gsend, ysend, send_sem, recv_sem
):
    s, b = lax.axis_index("slab"), lax.axis_index("brick")
    upper_s = (lax.rem(s + 1, N_SLAB), b)
    lower_s = (lax.rem(s + N_SLAB - 1, N_SLAB), b)
    upper_b = (s, lax.rem(b + 1, N_BRICK))
    lower_b = (s, lax.rem(b + N_BRICK - 1, N_BRICK))
    barrier = pltpu.get_barrier_semaphore()
    for peer in (upper_s, lower_s, upper_b, lower_b):
        pl.semaphore_signal(barrier, inc=1, device_id=peer, device_id_type=MESH)
    for g in range(16):
        source = glist[g]
        i, j, k = g // 8, g // 4 % 2, g % 4
        for c in range(3):
            gsend[i, j, k, c : c + 1, :] = pos[c, pl.ds(source, 1), :]
            gsend[i, j, k, 3 + c : 4 + c, :] = vel[c, pl.ds(source, 1), :]
        gsend[i, j, k, 6:7, :] = rad[pl.ds(source, 1), :]
        gsend[i, j, k, 7:8, :] = jnp.zeros((1, BLK), F32)
    for c in range(3):
        for ix in range(4):
            row = c * 4 + ix
            ysend[0, row : row + 1, :] = fluid[c, ix, 0:1, :]
            ysend[1, row : row + 1, :] = fluid[c, ix, 31:32, :]
    pl.semaphore_wait(barrier, 4)
    plan = (
        (gsend.at[1], ghosts.at[0], upper_s),
        (gsend.at[0], ghosts.at[1], lower_s),
        (gsend.at[:, 1], ghosts.at[2], upper_b),
        (gsend.at[:, 0], ghosts.at[3], lower_b),
        (fluid.at[:, 3], xlo, upper_s),
        (fluid.at[:, 0], xhi, lower_s),
        (ysend.at[1], ylo, upper_b),
        (ysend.at[0], yhi, lower_b),
    )
    copies = [
        pltpu.make_async_remote_copy(
            src_ref=src,
            dst_ref=dst,
            send_sem=send_sem.at[n],
            recv_sem=recv_sem.at[n],
            device_id=peer,
            device_id_type=MESH,
        )
        for n, (src, dst, peer) in enumerate(plan)
    ]
    for copy in copies:
        copy.start()
    for copy in copies:
        copy.wait()


def halo_exchange(glist, pos, vel, rad, fluid):
    sds = jax.ShapeDtypeStruct
    return pl.pallas_call(
        halo_kernel,
        out_shape=(
            sds((4, 2, 4, 8, BLK), F32),
            sds((3, 32, DEPTH), F32),
            sds((3, 32, DEPTH), F32),
            sds((16, DEPTH), F32),
            sds((16, DEPTH), F32),
        ),
        in_specs=[SMEM, VMEM, VMEM, VMEM, VMEM],
        out_specs=(VMEM,) * 5,
        scratch_shapes=[
            pltpu.VMEM((2, 2, 4, 8, BLK), F32),
            pltpu.VMEM((2, 16, DEPTH), F32),
            pltpu.SemaphoreType.DMA((8,)),
            pltpu.SemaphoreType.DMA((8,)),
        ],
        compiler_params=params(32, 0),
    )(glist, pos, vel, rad, fluid)


def contact_kernel(
    home,
    partner,
    pos,
    vel,
    rad,
    cell,
    route,
    ghosts,
    updated,
    slots,
    outgoing,
    cand,
    jfeat,
    ifeat,
    afeat,
    total,
    payload,
):
    for c in range(3):
        cand[0:NB, c, :] = pos[c]
        cand[0:NB, 3 + c, :] = vel[c]
    cand[0:NB, 6, :] = rad[...]
    cand[0:NB, 7, :] = jnp.zeros((NB, BLK), F32)
    cand[NB:CAND] = ghosts[...]
    total[...] = jnp.zeros_like(total)
    row = iota((8, BLK), 0)

    def features(n, _):
        q = cand[n]
        radius = q[6:7]
        q4 = jnp.where(row < 3, q, jnp.where(row == 3, radius, 0.0))
        square = q4 * q4
        p = jnp.sum(jnp.where(row == 3, square, -square), axis=0, keepdims=True)
        jt = jnp.where(row == 4, p, jnp.where(row == 5, 1.0, q4))
        it = jnp.where(row == 5, p, jnp.where(row == 4, 1.0, 2.0 * q4))
        speed = pltpu.roll(q, 5, 0)
        at = jnp.where(
            row < 3, stiffness * q - damping * speed, jnp.where(row == 3, 1.0, 0.0)
        )
        jh, jm, jl = (x.astype(F32) for x in split3(jt))
        ih, im, il = (x.astype(F32) for x in split3(it))
        ah, am, al = (x.astype(F32) for x in split3(at))
        jfeat[n] = jnp.concatenate([jh, jh, jm, jh, jl, jm], axis=0).astype(BF16)
        ifeat[n] = jnp.concatenate([ih, im, ih, il, ih, im], axis=0).astype(BF16)
        a = jnp.concatenate([ah, am, al, jnp.zeros_like(al)], axis=0).astype(BF16)
        afeat[n] = jnp.concatenate([a, a], axis=1)
        return 0

    lax.fori_loop(0, CAND, features, 0, unroll=8)

    def tile_sum(t):
        h, p = home[t], partner[t]
        s = lax.dot_general(
            jfeat[p], ifeat[h], (((0,), (0,)), ((), ())), preferred_element_type=F32
        )
        high, low = split2(jnp.maximum(s, 0.0))
        weight = jnp.concatenate([high, low], axis=0)
        out = jnp.dot(afeat[p], weight, preferred_element_type=F32)
        return h, out[0:8] + out[8:16] + out[16:24]

    def tiles(step, _):
        results = [tile_sum(step * 8 + n) for n in range(8)]
        for h, value in results:
            total[h] += value
        return 0

    lax.fori_loop(0, TILES // 8, tiles, 0)

    r = rad[...]
    mass = r * r * r
    weight_sum = total[:, 3, :]
    parts = [r]
    for c in range(3):
        a = stiffness * pos[c] - damping * vel[c]
        force = a * weight_sum - total[:, c, :]
        value = vel[c] + force / mass
        updated[c] = value
        parts.append(value)
    parts.append(cell[...].astype(F32) + 1.0)
    parts.append(jnp.zeros((NB, BLK), F32))
    for c, part in enumerate(parts):
        high, middle, low = split3(part)
        payload[c * NB : (c + 1) * NB, 0:BLK] = high
        payload[c * NB : (c + 1) * NB, BLK : 2 * BLK] = middle
        payload[c * NB : (c + 1) * NB, 2 * BLK : 3 * BLK] = low

    code = jnp.concatenate([route[...], route[...]], axis=1).astype(F32)
    lanes = jnp.broadcast_to(code, (BLK, BLK))
    across = jnp.transpose(lanes)
    sub, lane = iota((BLK, BLK), 0), iota((BLK, BLK), 1)
    earlier = (across == lanes) & (sub < NB) & (sub < lane % NB)
    before = jnp.sum(jnp.where(earlier, 1.0, 0.0), axis=0, keepdims=True)
    slot = code * CAP + before
    slots[...] = jnp.broadcast_to(slot, (8, BLK)).astype(jnp.int32)
    slot_i = slot.astype(jnp.int32)
    lane_row = iota((1, BLK), 1)
    upper_half = jnp.where(lane_row >= NB, 1, 0)
    key = jnp.concatenate([slot_i * 8 + 2 * g + upper_half for g in range(3)], axis=1)

    per = 192
    for part in range(CODES * SEND_ROWS // per):
        rho = iota((per, 3 * BLK), 0) + part * per
        q = rho % SEND_ROWS
        want = ((rho // SEND_ROWS) * CAP + q // 5) * 8 + q % 5
        want = jnp.where(q < 5 * CAP, want, -1)
        hot = jnp.where(want == key, 1.0, 0.0).astype(BF16)
        out = jnp.dot(hot, payload[...], preferred_element_type=F32)
        outgoing[part * per : (part + 1) * per, :] = (
            out[:, 0:BLK] + out[:, BLK : 2 * BLK] + out[:, 2 * BLK : 3 * BLK]
        )


def contacts(home, partner, pos, vel, rad, cell, route, ghosts):
    sds = jax.ShapeDtypeStruct
    return pl.pallas_call(
        contact_kernel,
        out_shape=(
            sds((3, NB, BLK), F32),
            sds((8, BLK), jnp.int32),
            sds((CODES * SEND_ROWS, BLK), F32),
        ),
        in_specs=[SMEM, SMEM] + [VMEM] * 6,
        out_specs=(VMEM,) * 3,
        scratch_shapes=[
            pltpu.VMEM((CAND, 8, BLK), F32),
            pltpu.VMEM((CAND, 48, BLK), BF16),
            pltpu.VMEM((CAND, 48, BLK), BF16),
            pltpu.VMEM((CAND, 32, 2 * BLK), BF16),
            pltpu.VMEM((NB, 8, BLK), F32),
            pltpu.VMEM((6 * NB, 3 * BLK), BF16),
        ],
        compiler_params=params(48),
    )(home, partner, pos, vel, rad, cell, route, ghosts)


def send_all(src, dst, send_sem, recv_sem, local_sem, rows, sign):
    s, b = lax.axis_index("slab"), lax.axis_index("brick")

    def region(index):
        return pl.ds(pl.multiple_of(index * rows, 8), rows)

    copies = []
    for turn in range(N_BRICK):
        brick = lax.rem(b + turn, N_BRICK)
        for o in range(3):
            slab = lax.rem(s + N_SLAB + sign * (o - 1), N_SLAB)
            n = turn * 3 + o
            source = src.at[region(o * N_BRICK + brick)]
            target = dst.at[region(o * N_BRICK + b)]
            if turn == 0 and o == 1:
                copies.append(pltpu.make_async_copy(source, target, local_sem))
            else:
                copies.append(
                    pltpu.make_async_remote_copy(
                        src_ref=source,
                        dst_ref=target,
                        send_sem=send_sem.at[n],
                        recv_sem=recv_sem.at[n],
                        device_id=(slab, brick),
                        device_id_type=MESH,
                    )
                )
    return copies


def greet_all(barrier):
    s, b = lax.axis_index("slab"), lax.axis_index("brick")
    for turn in range(N_BRICK):
        for o in range(3):
            if turn == 0 and o == 1:
                continue
            peer = (lax.rem(s + N_SLAB + o - 1, N_SLAB), lax.rem(b + turn, N_BRICK))
            pl.semaphore_signal(barrier, inc=1, device_id=peer, device_id_type=MESH)
    pl.semaphore_wait(barrier, 3 * N_BRICK - 1)


def route_kernel(src, dst, send_sem, recv_sem, local_sem):
    greet_all(pltpu.get_barrier_semaphore())
    copies = send_all(src, dst, send_sem, recv_sem, local_sem, SEND_ROWS, 1)
    for copy in copies:
        copy.start()
    for copy in copies:
        copy.wait()


def route_blocks(outgoing):
    return pl.pallas_call(
        route_kernel,
        out_shape=jax.ShapeDtypeStruct(outgoing.shape, F32),
        in_specs=[VMEM],
        out_specs=VMEM,
        scratch_shapes=[
            pltpu.SemaphoreType.DMA((CODES,)),
            pltpu.SemaphoreType.DMA((CODES,)),
            pltpu.SemaphoreType.DMA,
        ],
        compiler_params=params(32, 1),
    )(outgoing)


def return_kernel(slots, updated, src, out, back, send_sem, recv_sem, local_sem):
    greet_all(pltpu.get_barrier_semaphore())
    copies = send_all(src, back, send_sem, recv_sem, local_sem, BACK_ROWS, -1)
    for copy in copies:
        copy.start()
    for copy in copies:
        copy.wait()
    for n in range(NB):
        slot = slots[0, n]
        first = (slot // CAP) * BACK_ROWS + (slot % CAP) * 3
        for c in range(3):
            here = updated[c, n : n + 1, :]
            picked = back[pl.ds(first + c, 1), :]
            out[c, n : n + 1, :] = here + relaxation * (picked - here)


def return_answers(slots, updated, answers):
    return pl.pallas_call(
        return_kernel,
        out_shape=jax.ShapeDtypeStruct((3, NB, BLK), F32),
        in_specs=[SMEM, VMEM, VMEM],
        out_specs=VMEM,
        scratch_shapes=[
            pltpu.VMEM((CODES * BACK_ROWS, BLK), F32),
            pltpu.SemaphoreType.DMA((CODES,)),
            pltpu.SemaphoreType.DMA((CODES,)),
            pltpu.SemaphoreType.DMA,
        ],
        compiler_params=params(32, 2),
    )(slots, updated, answers)


def fluid_kernel(
    arrived, fluid, xlo, xhi, ylo, yhi, fluid_next, answers, blocks, sampled, acc, halves
):
    offset = []
    at = jnp.int32(0)
    valid = jnp.zeros((CODES, 1), F32)
    for k in range(CAP):
        cells = arrived[pl.ds(5 * k + 4, CODES, stride=SEND_ROWS), :]
        valid = valid + jnp.where(cells[:, 0:1] > 0.5, 1.0, 0.0)
    counted = valid.astype(jnp.int32)
    for d in range(CODES):
        offset.append(at)
        at = at + counted[d, 0]
    total = at
    blank = jnp.zeros((8, BLK), F32)
    for d in range(CODES):
        for k in range(CAP):
            base = d * SEND_ROWS + 5 * k
            blocks[offset[d] + k, 0:5, :] = arrived[base : base + 5, :]
    for n in range(CHUNK):
        blocks[total + n] = blank
    steps = (total + CHUNK - 1) // CHUNK
    acc[...] = jnp.zeros_like(acc)

    col_iota = iota((COLS, BLK), 0)
    z_sub = iota((DEPTH, BLK), 0)
    z_lane = iota((BLK, DEPTH), 1)

    def deposit(step, _):
        left, right = [], []
        for n in range(CHUNK):
            tile = blocks[step * CHUNK + n]
            cell = tile[4:5].astype(jnp.int32) - 1
            col, level = cell >> 9, cell & (DEPTH - 1)
            radius = tile[0:1]
            mass = radius * radius * radius
            hot = jnp.where(col_iota == col, 1.0, 0.0).astype(BF16)
            loads = [mass] + [mass * tile[1 + c : 2 + c] for c in range(3)]
            pieces = [split2(x) for x in loads]
            for which in range(2):
                left.append(jnp.concatenate([hot * p[which] for p in pieces], axis=0))
            depth_tile = jnp.broadcast_to(level.astype(F32), (BLK, BLK))
            column = jnp.transpose(depth_tile).astype(jnp.int32)
            wide = jnp.concatenate([column] * (DEPTH // BLK), axis=1)
            z_hot = jnp.where(wide == z_lane, 1.0, 0.0).astype(BF16)
            right += [z_hot, z_hot]
        acc[...] += jnp.dot(
            jnp.concatenate(left, axis=1),
            jnp.concatenate(right, axis=0),
            preferred_element_type=F32,
        )
        return 0

    lax.fori_loop(0, steps, deposit, 0)

    first_row = iota((32, DEPTH), 0) == 0
    last_row = iota((32, DEPTH), 0) == 31
    first_z = iota((32, DEPTH), 1) == 0
    last_z = iota((32, DEPTH), 1) == DEPTH - 1
    for ix in range(4):
        base = ix * 32
        volume = acc[base : base + 32, :]
        for c in range(3):
            f = fluid[c, ix]
            below = xlo[c] if ix == 0 else fluid[c, ix - 1]
            above = xhi[c] if ix == 3 else fluid[c, ix + 1]
            row = c * 4 + ix
            near = jnp.where(first_row, ylo[row : row + 1, :], pltpu.roll(f, 1, 0))
            far = jnp.where(last_row, yhi[row : row + 1, :], pltpu.roll(f, 31, 0))
            down = jnp.where(first_z, 0.0, pltpu.roll(f, 1, 1))
            up = jnp.where(last_z, 0.0, pltpu.roll(f, DEPTH - 1, 1))
            around = above + below
            around = around + far + near
            around = around + up + down
            start = (c + 1) * COLS + base
            momentum = acc[start : start + 32, :]
            value = f + viscosity * (around - 6.0 * f) + coupling * (momentum - volume * f)
            fluid_next[c, ix] = value
            high, low = split2(value)
            halves[c * COLS + base : c * COLS + base + 32, :] = high
            halves[(3 + c) * COLS + base : (3 + c) * COLS + base + 32, :] = low

    def sample(step, _):
        hots, cols = [], []
        for n in range(CHUNK):
            tile = blocks[step * CHUNK + n]
            cell = tile[4:5].astype(jnp.int32) - 1
            col, level = cell >> 9, cell & (DEPTH - 1)
            hots.append(jnp.where(z_sub == level, 1.0, 0.0).astype(BF16))
            cols.append(col_iota == col)
        along = jnp.dot(
            halves[...], jnp.concatenate(hots, axis=1), preferred_element_type=F32
        )
        for n in range(CHUNK):
            for c in range(3):
                part = along[:, n * BLK : (n + 1) * BLK]
                both = part[c * COLS : (c + 1) * COLS] + part[(3 + c) * COLS : (4 + c) * COLS]
                value = jnp.sum(jnp.where(cols[n], both, 0.0), axis=0, keepdims=True)
                sampled[step * CHUNK + n, c : c + 1, :] = value
        return 0

    lax.fori_loop(0, steps, sample, 0)
    for n in range(CAP + CHUNK):
        sampled[total + n] = blank
    for d in range(CODES):
        for k in range(CAP):
            base = d * BACK_ROWS + 3 * k
            answers[base : base + 3, :] = sampled[offset[d] + k, 0:3, :]
        answers[d * BACK_ROWS + 3 * CAP : (d + 1) * BACK_ROWS, :] = jnp.zeros(
            (BACK_ROWS - 3 * CAP, BLK), F32
        )


def advance(arrived, fluid, xlo, xhi, ylo, yhi):
    sds = jax.ShapeDtypeStruct
    room = CODES * CAP + 2 * CAP
    return pl.pallas_call(
        fluid_kernel,
        out_shape=(sds((3, 4, 32, DEPTH), F32), sds((CODES * BACK_ROWS, BLK), F32)),
        in_specs=[VMEM] * 6,
        out_specs=(VMEM,) * 2,
        scratch_shapes=[
            pltpu.VMEM((room, 8, BLK), F32),
            pltpu.VMEM((room, 8, BLK), F32),
            pltpu.VMEM((4 * COLS, DEPTH), F32),
            pltpu.VMEM((6 * COLS, DEPTH), BF16),
        ],
        compiler_params=params(48),
    )(arrived, fluid, xlo, xhi, ylo, yhi)


def on_device(
    positions, velocities, radii, cell_of, block_route, ghost_list, tile_home, tile_partner, fluid
):
    pos = jnp.transpose(positions, (1, 0, 2))
    vel = jnp.transpose(velocities, (1, 0, 2))
    route = jnp.transpose(block_route, (1, 0))
    ghosts, xlo, xhi, ylo, yhi = halo_exchange(ghost_list, pos, vel, radii, fluid)
    updated, slots, outgoing = contacts(
        tile_home, tile_partner, pos, vel, radii, cell_of, route, ghosts.reshape(32, 8, BLK)
    )
    arrived = route_blocks(outgoing)
    fluid_next, answers = advance(arrived, fluid, xlo, xhi, ylo, yhi)
    velocity_next = return_answers(slots, updated, answers)
    return jnp.transpose(velocity_next, (1, 0, 2)), fluid_next


def solution(mesh):
    placed = (
        P(("slab", "brick"), None, None),
        P(("slab", "brick"), None, None),
        P(("slab", "brick"), None),
        P(("slab", "brick"), None),
        P(("slab", "brick"), None),
        P(("slab", "brick")),
        P(("slab", "brick")),
        P(("slab", "brick")),
        P(None, "slab", "brick", None),
    )
    return jax.shard_map(
        on_device,
        mesh=mesh,
        in_specs=placed,
        out_specs=(P(("slab", "brick"), None, None), P(None, "slab", "brick", None)),
        check_vma=False,
    )
```

time: 355 us -> 109 us (0.31)
  matrix products: 132 us -> 0 us
  other arithmetic: 115 us -> 0 us
  Pallas kernels: 0 us -> 103 us
  waiting for transfers between devices: 31.8 us -> 0 us
  local copies, waits for them, and re-layouts: 36.6 us -> 5 us
  starting transfers between devices: 23.8 us -> 0 us
  blocking collectives: 10.9 us -> 0 us
    dot_general x70 -> x0, matrix products: 132 us -> none  [the longest x27 83.1 us: first_dims(): lax.dot_general(left, right, (((0,), (0,)), ((), ())), precision=highest)]
    pallas_call x0 -> x5, Pallas kernels: none -> 103 us  [the longest x1 39.2 us: return_answers(): pl.pallas_call(return_kernel, out_shape=jax.ShapeDtypeStruct((3, NB, BLK)...]
    mul x73 -> x0, other arithmetic: 70.1 us -> none  [the longest x18 69.8 us: deposit(): left = (loads[:, :, None] * col_hot[:, None, :]).reshape(-1, 4 * columns)]
    reduce_sum x43 -> x0, other arithmetic: 32.3 us -> none  [the longest x8 14.9 us: tile_forces(): spring = jnp.sum(weight[:, None] * offsets, axis=3)]
    ppermute x12 -> x0, waiting for transfers between devices: 31.8 us -> none  [the longest x6 17.4 us: padded_2(): after = lax.ppermute(first, axis, down)]
    ppermute x12 -> x0, starting transfers between devices: 19.5 us -> none  [the longest x6 9.88 us: padded_2(): after = lax.ppermute(first, axis, down)]
    while x90 -> x0, local copies, waits for them, and re-layouts: 12.2 us -> none
    all_to_all x1 -> x0, blocking collectives: 10.9 us -> none  [on_device(): lax.all_to_all(answers, 'brick', split_axis=1, concat_axis=1, tiled=True)]
  transfers between devices with their start and end apart: 13 -> 0, of which waited for: 6 -> 0; matrix products, arithmetic and copies ran while one was open for 15% -> 0% of each run, Pallas kernels for 0% -> 0%
where the time goes in v1:
time: 109 us
  Pallas kernels  103 us (94%)
  local copies, waits for them, and re-layouts  5 us (5%)
    pallas_call x1, Pallas kernels, return_answers(): pl.pallas_call(return_kernel, out_shape=jax.ShapeDtypeStruct((3, NB, BLK)...  39.2 us
    pallas_call x1, Pallas kernels, advance(): pl.pallas_call(fluid_kernel, out_shape=(sds((3, 4, 32, DEPTH), F32), sds(...  25.3 us
    pallas_call x1, Pallas kernels, route_blocks(): pl.pallas_call(route_kernel, out_shape=jax.ShapeDtypeStruct(outgoing.shap...  14.6 us
    pallas_call x1, Pallas kernels, halo_exchange(): pl.pallas_call(halo_kernel, out_shape=(sds((4, 2, 4, 8, BLK), F32), sds((...  14.5 us
    pallas_call x1, Pallas kernels, contacts(): pl.pallas_call(contact_kernel, out_shape=(sds((3, NB, BLK), F32), sds((8,...  9.2 us
    unnamed x27, local copies, waits for them, and re-layouts  5 us

profile of v1, /device:TPU:1, one launch (start us, length us, event | category | flops | bytes accessed | tf_op | source)
XLA Modules:
  0.0 108.6 jit_solution(6861097965396673216)
XLA Ops:
  0.6 0.0 copy-start.9
  0.6 0.6 copy-done.9
  1.3 1.1 %copy-done = f32[3,4,32,512]{3,2,1,0:T(8,128)S(1)} copy-done((f32[3,4,32,512]{3,2,1,0:T(8,128)S(1)}, f32[3,4,32,512]{3,2,1,0:T(8,128)}, u32[]{:S(2)}) %copy-start) | copy-done | bytes 786456
  2.4 0.9 copy-done.2
  3.3 0.9 copy-done.4
  4.2 0.8 copy-done.6
  5.0 0.0 copy-start.10
  5.0 0.0 copy-start.11
  5.0 0.0 copy-start.12
  5.0 14.5 %shard_map.104 = (f32[4,2,4,8,128]{4,3,2,1,0:T(8,128)S(1)}, f32[3,32,512]{2,1,0:T(8,128)S(1)}, f32[3,32,512]{2,1,0:T(8,128)S(1)}, f32[16,512]{1,0:T(8,128)S(1)}, f32[16,512]{1,0:T(8,128)S(1)}) custom-call(s32[16]{0:T(128)S(1)} %copy-done.9, f32[3,64,128]{2,1,0:T(8,128)S(1)} %bitcast.5, f32[3,64,128]{2,1,0:T(8,128)S(1)} %bitcast.7, f32[64,128]{1,0:T(8,128)S(1)} %copy-done.6, ...), custom_call_target="tpu_custom_call" | custom-call | tf_op jit(solution)/shard_map/pallas_call | solution.py:116
  19.5 0.0 copy-start.1
  19.5 0.0 copy-done.3
  19.5 0.0 copy-done.5
  19.5 0.0 copy-done.7
  19.5 0.0 copy-done.8
  19.5 0.0 copy-done.10
  19.5 0.0 copy-done.11
  19.5 0.0 copy-done.12
  19.6 9.2 %shard_map.105 = (f32[3,64,128]{2,1,0:T(8,128)S(1)}, s32[8,128]{1,0:T(8,128)S(1)}, f32[768,128]{1,0:T(8,128)S(1)}) custom-call(s32[128]{0:T(128)S(1)} %copy-done.10, s32[128]{0:T(128)S(1)} %copy-done.11, f32[3,64,128]{2,1,0:T(8,128)S(1)} %bitcast.6, f32[3,64,128]{2,1,0:T(8,128)S(1)} %bitcast.8, f32[64,128]{1,0:T(8,128)S(1)} %copy-done.7, ...), custom_call_target="tpu_custom_call" | custom-call | tf_op jit(solution)/shard_map/pallas_call | solution.py:252
  28.8 14.6 %shard_map.106.arrived = f32[768,128]{1,0:T(8,128)S(1)} custom-call(f32[768,128]{1,0:T(8,128)S(1)} %get-tuple-element.15.src), custom_call_target="tpu_custom_call" | custom-call | tf_op jit(solution)/shard_map/pallas_call | solution.py:324
  43.4 0.0 copy-done.1
  43.4 25.3 %shard_map.107 = (f32[3,4,32,512]{3,2,1,0:T(8,128)}, f32[576,128]{1,0:T(8,128)S(1)}) custom-call(f32[768,128]{1,0:T(8,128)S(1)} %shard_map.106.arrived, f32[3,4,32,512]{3,2,1,0:T(8,128)S(1)} %copy-done.1, f32[3,32,512]{2,1,0:T(8,128)S(1)} %get-tuple-element.16.xlo, f32[3,32,512]{2,1,0:T(8,128)S(1)} %get-tuple-element.17.xhi, ...), custom_call_target="tpu_custom_call" | custom-call | tf_op jit(solution)/shard_map/pallas_call | solution.py:486
  68.7 39.2 %shard_map.108 = f32[3,64,128]{2,1,0:T(8,128)S(1)} custom-call(s32[8,128]{1,0:T(8,128)S(1)} %get-tuple-element.13.slots, f32[3,64,128]{2,1,0:T(8,128)S(1)} %get-tuple-element.14.updated, f32[576,128]{1,0:T(8,128)S(1)} %get-tuple-element.20.src), custom_call_target="tpu_custom_call" | custom-call | tf_op jit(solution)/shard_map/pallas_call | solution.py:355
  107.9 0.6 copy.12
  (8 shorter events, 0.0 us)
Async XLA Ops:
  0.6 0.7 copy-start.9
  1.3 1.1 %copy-start = (f32[3,4,32,512]{3,2,1,0:T(8,128)S(1)}, f32[3,4,32,512]{3,2,1,0:T(8,128)}, u32[]{:S(2)}) copy-start(f32[3,4,32,512]{3,2,1,0:T(8,128)} %fluid.3) | copy-start | bytes 2359300
  2.4 0.9 copy-start.2
  3.3 0.9 copy-start.4
  4.2 0.8 copy-start.6
  5.0 14.5 %copy-start.3 = (f32[64,3,128]{2,0,1:T(8,128)S(1)}, f32[64,3,128]{2,0,1:T(8,128)}, u32[]{:S(2)}) copy-start(f32[64,3,128]{2,0,1:T(8,128)} %param.9) | copy-start | bytes 294916
  5.0 14.5 %copy-start.5 = (f32[64,3,128]{2,0,1:T(8,128)S(1)}, f32[64,3,128]{2,0,1:T(8,128)}, u32[]{:S(2)}) copy-start(f32[64,3,128]{2,0,1:T(8,128)} %param.10) | copy-start | bytes 294916
  5.0 14.5 %copy-start.7 = (f32[64,128]{1,0:T(8,128)S(1)}, f32[64,128]{1,0:T(8,128)}, u32[]{:S(2)}) copy-start(f32[64,128]{1,0:T(8,128)} %rad.3) | copy-start | bytes 98308
  5.0 14.5 %copy-start.8 = (s32[64,128]{1,0:T(8,128)S(1)}, s32[64,128]{1,0:T(8,128)}, u32[]{:S(2)}) copy-start(s32[64,128]{1,0:T(8,128)} %cell.1) | copy-start | bytes 98308
  5.0 14.5 %copy-start.10 = (s32[128]{0:T(128)S(1)}, s32[128]{0:T(128)}, u32[]{:S(2)}) copy-start(s32[128]{0:T(128)} %home.1) | copy-start | bytes 1540
  5.0 14.5 %copy-start.11 = (s32[128]{0:T(128)S(1)}, s32[128]{0:T(128)}, u32[]{:S(2)}) copy-start(s32[128]{0:T(128)} %partner.1) | copy-start | bytes 1540
  5.0 14.5 %copy-start.12 = (s32[64,1]{0,1:T(1,128)S(1)}, s32[64,1]{0,1:T(1,128)}, u32[]{:S(2)}) copy-start(s32[64,1]{0,1:T(1,128)} %param.13) | copy-start | bytes 772
  19.5 23.9 %copy-start.1 = (f32[3,4,32,512]{3,2,1,0:T(8,128)S(1)}, f32[3,4,32,512]{3,2,1,0:T(8,128)}, u32[]{:S(2)}) copy-start(f32[3,4,32,512]{3,2,1,0:T(8,128)} %fluid.3) | copy-start | bytes 2359300

commit v2 on v1

v2 whole, which is shorter than its diff:
```python
import functools

import jax
import jax.numpy as jnp
from jax import lax
from jax.experimental import pallas as pl
from jax.experimental.pallas import tpu as pltpu
from jax.sharding import PartitionSpec as P

stiffness = 0.01
damping = 0.005
viscosity = 0.1
coupling = 0.5
relaxation = 0.5

MESH = pl.DeviceIdType.MESH
F32 = jnp.float32
BF16 = jnp.bfloat16
VMEM = pl.BlockSpec(memory_space=pltpu.VMEM)
SMEM = pl.BlockSpec(memory_space=pltpu.SMEM)
HBM = pl.BlockSpec(memory_space=pltpu.HBM)

N_SLAB = 16
N_BRICK = 8
NB = 64
BLK = 128
TILES = 128
CAND = 96
CODES = 24
CAP = 6
EARLY_ROWS = 16
LATE_ROWS = 24
BACK_ROWS = 24
COLS = 128
DEPTH = 512
BIG = 16
SMALL = 4


def iota(shape, dim, dtype=jnp.int32):
    return lax.broadcasted_iota(jnp.int32, shape, dim).astype(dtype)


def split3(x):
    high = x.astype(BF16)
    rest = x - high.astype(F32)
    middle = rest.astype(BF16)
    low = (rest - middle.astype(F32)).astype(BF16)
    return high, middle, low


def split2(x):
    high = x.astype(BF16)
    return high, (x - high.astype(F32)).astype(BF16)


def params(mib, collective_id=None):
    return pltpu.CompilerParams(
        vmem_limit_bytes=mib << 20,
        collective_id=collective_id,
        has_side_effects=collective_id is not None,
    )


def particle_kernel(
    glist_h,
    home_h,
    partner_h,
    home_v,
    pos_h,
    vel_h,
    rad_h,
    cell_h,
    route_h,
    fluid_h,
    updated,
    slots,
    early,
    late,
    xlo,
    xhi,
    ylo,
    yhi,
    glist,
    home,
    partner,
    pos,
    vel,
    rad,
    cell,
    route,
    fluid,
    gsend,
    ghosts,
    ysend,
    cand,
    jfeat,
    ifeat,
    afeat,
    terms,
    payload,
    out_early,
    out_late,
    load_sem,
    halo_send,
    halo_recv,
    early_send,
    early_recv,
    late_send,
    late_recv,
    local_sem,
):
    s, b = lax.axis_index("slab"), lax.axis_index("brick")
    upper_s = (lax.rem(s + 1, N_SLAB), b)
    lower_s = (lax.rem(s + N_SLAB - 1, N_SLAB), b)
    upper_b = (s, lax.rem(b + 1, N_BRICK))
    lower_b = (s, lax.rem(b + N_BRICK - 1, N_BRICK))
    pairs = (
        (glist_h, glist),
        (pos_h, pos),
        (vel_h, vel),
        (rad_h, rad),
        (route_h, route),
        (cell_h, cell),
        (home_h, home),
        (partner_h, partner),
        (fluid_h, fluid),
    )
    loads = [pltpu.make_async_copy(a, z, load_sem.at[n]) for n, (a, z) in enumerate(pairs)]
    for load in loads:
        load.start()
    barrier = pltpu.get_barrier_semaphore()
    greet_all(barrier)
    for load in loads[:4]:
        load.wait()
    for g in range(16):
        source = glist[g]
        i, j, k = g // 8, g // 4 % 2, g % 4
        for c in range(3):
            gsend[i, j, k, c : c + 1, :] = pos[c, pl.ds(source, 1), :]
            gsend[i, j, k, 3 + c : 4 + c, :] = vel[c, pl.ds(source, 1), :]
        gsend[i, j, k, 6:7, :] = rad[pl.ds(source, 1), :]
        gsend[i, j, k, 7:8, :] = jnp.zeros((1, BLK), F32)
    pl.semaphore_wait(barrier, 3 * N_BRICK - 1)
    plan = (
        (gsend.at[1], ghosts.at[0], upper_s),
        (gsend.at[0], ghosts.at[1], lower_s),
        (gsend.at[:, 1], ghosts.at[2], upper_b),
        (gsend.at[:, 0], ghosts.at[3], lower_b),
        (fluid.at[:, 3], xlo, upper_s),
        (fluid.at[:, 0], xhi, lower_s),
        (ysend.at[1], ylo, upper_b),
        (ysend.at[0], yhi, lower_b),
    )
    halos = [
        pltpu.make_async_remote_copy(
            src_ref=src,
            dst_ref=dst,
            send_sem=halo_send.at[n],
            recv_sem=halo_recv.at[n],
            device_id=peer,
            device_id_type=MESH,
        )
        for n, (src, dst, peer) in enumerate(plan)
    ]
    for copy in halos[:4]:
        copy.start()

    for load in loads[4:6]:
        load.wait()
    code = jnp.concatenate([route[...], route[...]], axis=1).astype(F32)
    lanes = jnp.broadcast_to(code, (BLK, BLK))
    across = jnp.transpose(lanes)
    sub, lane = iota((BLK, BLK), 0), iota((BLK, BLK), 1)
    earlier = (across == lanes) & (sub < NB) & (sub < lane % NB)
    before = jnp.sum(jnp.where(earlier, 1.0, 0.0), axis=0, keepdims=True)
    slot = (code * CAP + before).astype(jnp.int32)
    slots[...] = jnp.broadcast_to(slot, (8, BLK))
    upper_half = jnp.where(iota((1, BLK), 1) >= NB, 1, 0)

    def lay_out(channels, rows, out, per):
        groups = (len(channels) + 1) // 2
        for c, part in enumerate(channels):
            high, middle, low = split3(part)
            payload[c * NB : (c + 1) * NB, 0:BLK] = high
            payload[c * NB : (c + 1) * NB, BLK : 2 * BLK] = middle
            payload[c * NB : (c + 1) * NB, 2 * BLK : 3 * BLK] = low
        count = len(channels)
        if count % 2:
            payload[count * NB : (count + 1) * NB, :] = jnp.zeros((NB, 3 * BLK), BF16)
        key = [slot * 8 + 2 * g + upper_half for g in range(groups)]
        key = jnp.concatenate(key, axis=1) if groups > 1 else key[0]

        def piece(part, _):
            rho = iota((per, groups * BLK), 0) + part * per
            q = rho % rows
            want = ((rho // rows) * CAP + q // count) * 8 + q % count
            want = jnp.where(q < count * CAP, want, -1)
            hot = jnp.where(want == key, 1.0, 0.0).astype(BF16)
            got = jnp.dot(hot, payload[0 : groups * BLK, :], preferred_element_type=F32)
            out[pl.ds(pl.multiple_of(part * per, 8), per), :] = (
                got[:, 0:BLK] + got[:, BLK : 2 * BLK] + got[:, 2 * BLK : 3 * BLK]
            )
            return 0

        lax.fori_loop(0, CODES * rows // per, piece, 0)

    lay_out([rad[...], cell[...].astype(F32) + 1.0], EARLY_ROWS, out_early, 192)
    first = send_all(out_early, early, early_send, early_recv, local_sem.at[0], EARLY_ROWS, 1)
    for copy in first:
        copy.start()

    loads[8].wait()
    for c in range(3):
        for ix in range(4):
            at = c * 4 + ix
            ysend[0, at : at + 1, :] = fluid[c, ix, 0:1, :]
            ysend[1, at : at + 1, :] = fluid[c, ix, 31:32, :]
    for copy in halos[4:]:
        copy.start()

    for c in range(3):
        cand[0:NB, c, :] = pos[c]
        cand[0:NB, 3 + c, :] = vel[c]
    cand[0:NB, 6, :] = rad[...]
    cand[0:NB, 7, :] = jnp.zeros((NB, BLK), F32)
    row = iota((8, BLK), 0)

    def features(n, _):
        q = cand[n]
        q4 = jnp.where(row < 3, q, jnp.where(row == 3, q[6:7], 0.0))
        square = q4 * q4
        p = jnp.sum(jnp.where(row == 3, square, -square), axis=0, keepdims=True)
        jt = jnp.where(row == 4, p, jnp.where(row == 5, 1.0, q4))
        it = jnp.where(row == 5, p, jnp.where(row == 4, 1.0, 2.0 * q4))
        speed = pltpu.roll(q, 5, 0)
        at = jnp.where(
            row < 3, stiffness * q - damping * speed, jnp.where(row == 3, 1.0, 0.0)
        )
        jh, jm, jl = (x.astype(F32) for x in split3(jt))
        ih, im, il = (x.astype(F32) for x in split3(it))
        ah, am, al = (x.astype(F32) for x in split3(at))
        jfeat[n] = jnp.concatenate([jh, jh, jm, jh, jl, jm], axis=0).astype(BF16)
        ifeat[n] = jnp.concatenate([ih, im, ih, il, ih, im], axis=0).astype(BF16)
        a = jnp.concatenate([ah, am, al, jnp.zeros_like(al)], axis=0).astype(BF16)
        afeat[n] = jnp.concatenate([a, a], axis=1)
        return 0

    def features_of(step, _):
        for n in range(8):
            features(step * 8 + n, 0)
        return 0

    lax.fori_loop(0, NB // 8, features_of, 0)
    for copy in halos[:4]:
        copy.wait()
    for n in range(4):
        cand[NB + 8 * n : NB + 8 * (n + 1)] = ghosts[n].reshape(8, 8, BLK)
    lax.fori_loop(NB // 8, CAND // 8, features_of, 0)
    for load in loads[6:8]:
        load.wait()

    def tile_sum(t):
        h, p = home[t], partner[t]
        near = lax.dot_general(
            jfeat[p], ifeat[h], (((0,), (0,)), ((), ())), preferred_element_type=F32
        )
        high, low = split2(jnp.maximum(near, 0.0))
        weight = jnp.concatenate([high, low], axis=0)
        out = jnp.dot(afeat[p], weight, preferred_element_type=F32)
        return out[0:8] + out[8:16] + out[16:24]

    def tiles(step, _):
        for n, value in enumerate([tile_sum(step * 8 + n) for n in range(8)]):
            terms[step * 8 + n] = value
        return 0

    lax.fori_loop(0, TILES // 8, tiles, 0)

    belongs = jnp.where(iota((NB, TILES), 0) == home_v[...], 1.0, 0.0).astype(BF16)

    def gathered(c):
        pieces = jnp.concatenate(split3(terms[:, c, :]), axis=1)
        got = jnp.dot(belongs, pieces, preferred_element_type=F32)
        return got[:, 0:BLK] + got[:, BLK : 2 * BLK] + got[:, 2 * BLK : 3 * BLK]

    r = rad[...]
    mass = r * r * r
    weight_sum = gathered(3)
    values = []
    for c in range(3):
        a = stiffness * pos[c] - damping * vel[c]
        value = vel[c] + (a * weight_sum - gathered(c)) / mass
        updated[c] = value
        values.append(value)
    lay_out(values, LATE_ROWS, out_late, 192)
    second = send_all(out_late, late, late_send, late_recv, local_sem.at[1], LATE_ROWS, 1)
    for copy in second:
        copy.start()
    for copy in halos[4:] + first + second:
        copy.wait()


def particles(home, partner, pos, vel, rad, cell, route, glist, fluid):
    sds = jax.ShapeDtypeStruct
    return pl.pallas_call(
        particle_kernel,
        out_shape=(
            sds((3, NB, BLK), F32),
            sds((8, BLK), jnp.int32),
            sds((CODES * EARLY_ROWS, BLK), F32),
            sds((CODES * LATE_ROWS, BLK), F32),
            sds((3, 32, DEPTH), F32),
            sds((3, 32, DEPTH), F32),
            sds((16, DEPTH), F32),
            sds((16, DEPTH), F32),
        ),
        in_specs=[HBM] * 3 + [VMEM] + [HBM] * 6,
        out_specs=(VMEM,) * 8,
        scratch_shapes=[
            pltpu.SMEM((16,), jnp.int32),
            pltpu.SMEM((TILES,), jnp.int32),
            pltpu.SMEM((TILES,), jnp.int32),
            pltpu.VMEM((3, NB, BLK), F32),
            pltpu.VMEM((3, NB, BLK), F32),
            pltpu.VMEM((NB, BLK), F32),
            pltpu.VMEM((NB, BLK), jnp.int32),
            pltpu.VMEM((1, NB), jnp.int32),
            pltpu.VMEM((3, 4, 32, DEPTH), F32),
            pltpu.VMEM((2, 2, 4, 8, BLK), F32),
            pltpu.VMEM((4, 2, 4, 8, BLK), F32),
            pltpu.VMEM((2, 16, DEPTH), F32),
            pltpu.VMEM((CAND, 8, BLK), F32),
            pltpu.VMEM((CAND, 48, BLK), BF16),
            pltpu.VMEM((CAND, 48, BLK), BF16),
            pltpu.VMEM((CAND, 32, 2 * BLK), BF16),
            pltpu.VMEM((TILES, 8, BLK), F32),
            pltpu.VMEM((4 * NB, 3 * BLK), BF16),
            pltpu.VMEM((CODES * EARLY_ROWS, BLK), F32),
            pltpu.VMEM((CODES * LATE_ROWS, BLK), F32),
            pltpu.SemaphoreType.DMA((9,)),
            pltpu.SemaphoreType.DMA((8,)),
            pltpu.SemaphoreType.DMA((8,)),
            pltpu.SemaphoreType.DMA((CODES,)),
            pltpu.SemaphoreType.DMA((CODES,)),
            pltpu.SemaphoreType.DMA((CODES,)),
            pltpu.SemaphoreType.DMA((CODES,)),
            pltpu.SemaphoreType.DMA((2,)),
        ],
        compiler_params=params(40, 0),
    )(glist, home, partner, home.reshape(1, TILES), pos, vel, rad, cell, route, fluid)


def send_all(src, dst, send_sem, recv_sem, local_sem, rows, sign):
    s, b = lax.axis_index("slab"), lax.axis_index("brick")

    def region(index):
        return pl.ds(pl.multiple_of(index * rows, 8), rows)

    copies = []
    for turn in range(N_BRICK):
        brick = lax.rem(b + turn, N_BRICK)
        for o in range(3):
            slab = lax.rem(s + N_SLAB + sign * (o - 1), N_SLAB)
            n = turn * 3 + o
            source = src.at[region(o * N_BRICK + brick)]
            target = dst.at[region(o * N_BRICK + b)]
            if turn == 0 and o == 1:
                copies.append(pltpu.make_async_copy(source, target, local_sem))
            else:
                copies.append(
                    pltpu.make_async_remote_copy(
                        src_ref=source,
                        dst_ref=target,
                        send_sem=send_sem.at[n],
                        recv_sem=recv_sem.at[n],
                        device_id=(slab, brick),
                        device_id_type=MESH,
                    )
                )
    return copies


def greet_all(barrier):
    s, b = lax.axis_index("slab"), lax.axis_index("brick")
    for turn in range(N_BRICK):
        for o in range(3):
            if turn == 0 and o == 1:
                continue
            peer = (lax.rem(s + N_SLAB + o - 1, N_SLAB), lax.rem(b + turn, N_BRICK))
            pl.semaphore_signal(barrier, inc=1, device_id=peer, device_id_type=MESH)


def return_kernel(slots, updated, src, out, back, send_sem, recv_sem, local_sem):
    barrier = pltpu.get_barrier_semaphore()
    greet_all(barrier)
    pl.semaphore_wait(barrier, 3 * N_BRICK - 1)
    copies = send_all(src, back, send_sem, recv_sem, local_sem, BACK_ROWS, -1)
    for copy in copies:
        copy.start()
    for copy in copies:
        copy.wait()
    for n in range(NB):
        slot = slots[0, n]
        first = (slot // CAP) * BACK_ROWS + (slot % CAP) * 3
        for c in range(3):
            here = updated[c, n : n + 1, :]
            picked = back[pl.ds(first + c, 1), :]
            out[c, n : n + 1, :] = here + relaxation * (picked - here)


def return_answers(slots, updated, answers):
    return pl.pallas_call(
        return_kernel,
        out_shape=jax.ShapeDtypeStruct((3, NB, BLK), F32),
        in_specs=[SMEM, VMEM, VMEM],
        out_specs=VMEM,
        scratch_shapes=[
            pltpu.VMEM((CODES * BACK_ROWS, BLK), F32),
            pltpu.SemaphoreType.DMA((CODES,)),
            pltpu.SemaphoreType.DMA((CODES,)),
            pltpu.SemaphoreType.DMA,
        ],
        compiler_params=params(32, 1),
    )(slots, updated, answers)


def fluid_kernel(
    early,
    late,
    fluid_h,
    xlo,
    xhi,
    ylo,
    yhi,
    next_h,
    answers,
    fluid,
    fluid_next,
    blocks,
    sampled,
    acc,
    halves,
    load_sem,
    store_sem,
):
    load = pltpu.make_async_copy(fluid_h, fluid, load_sem)
    load.start()
    valid = jnp.zeros((CODES, 1), F32)
    for k in range(CAP):
        cells = early[pl.ds(2 * k + 1, CODES, stride=EARLY_ROWS), :]
        valid = valid + jnp.where(cells[:, 0:1] > 0.5, 1.0, 0.0)
    counted = valid.astype(jnp.int32)
    offset = []
    total = jnp.int32(0)
    for d in range(CODES):
        offset.append(total)
        total = total + counted[d, 0]
    acc[...] = jnp.zeros_like(acc)
    blank = jnp.zeros((8, BLK), F32)
    for d in range(CODES):
        for k in range(CAP):
            base = d * EARLY_ROWS + 2 * k
            blocks[offset[d] + k, 0:2, :] = early[base : base + 2, :]
            base = d * LATE_ROWS + 3 * k
            blocks[offset[d] + k, 2:5, :] = late[base : base + 3, :]
    for n in range(CAP):
        blocks[total + n] = blank
    big = total // BIG
    small = (total - big * BIG + SMALL - 1) // SMALL

    def in_chunks(run):
        def big_step(step, _):
            run(step * BIG, BIG)
            return 0

        def small_step(step, _):
            run(big * BIG + step * SMALL, SMALL)
            return 0

        lax.fori_loop(0, big, big_step, 0)
        lax.fori_loop(0, small, small_step, 0)

    col_iota = iota((COLS, BLK), 0)
    z_sub = iota((DEPTH, BLK), 0)
    z_lane = iota((BLK, DEPTH), 1)

    def deposit(first, count):
        left, right = [[], []], []
        for n in range(count):
            tile = blocks[first + n]
            cell = tile[1:2].astype(jnp.int32) - 1
            col, level = cell >> 9, cell & (DEPTH - 1)
            radius = tile[0:1]
            mass = radius * radius * radius
            hot = jnp.where(col_iota == col, 1.0, 0.0).astype(BF16)
            pieces = [split2(x) for x in [mass] + [mass * tile[2 + c : 3 + c] for c in range(3)]]
            for which in range(2):
                left[which].append(jnp.concatenate([hot * p[which] for p in pieces], axis=0))
            depth_tile = jnp.broadcast_to(level.astype(F32), (BLK, BLK))
            column = jnp.transpose(depth_tile).astype(jnp.int32)
            wide = jnp.concatenate([column] * (DEPTH // BLK), axis=1)
            right.append(jnp.where(wide == z_lane, 1.0, 0.0).astype(BF16))
        tall = jnp.concatenate([jnp.concatenate(x, axis=1) for x in left], axis=0)
        both = jnp.dot(tall, jnp.concatenate(right, axis=0), preferred_element_type=F32)
        acc[...] += both[0 : 4 * COLS] + both[4 * COLS : 8 * COLS]

    in_chunks(deposit)
    load.wait()

    first_row = iota((32, DEPTH), 0) == 0
    last_row = iota((32, DEPTH), 0) == 31
    first_z = iota((32, DEPTH), 1) == 0
    last_z = iota((32, DEPTH), 1) == DEPTH - 1
    for ix in range(4):
        base = ix * 32
        volume = acc[base : base + 32, :]
        for c in range(3):
            f = fluid[c, ix]
            below = xlo[c] if ix == 0 else fluid[c, ix - 1]
            above = xhi[c] if ix == 3 else fluid[c, ix + 1]
            row = c * 4 + ix
            near = jnp.where(first_row, ylo[row : row + 1, :], pltpu.roll(f, 1, 0))
            far = jnp.where(last_row, yhi[row : row + 1, :], pltpu.roll(f, 31, 0))
            down = jnp.where(first_z, 0.0, pltpu.roll(f, 1, 1))
            up = jnp.where(last_z, 0.0, pltpu.roll(f, DEPTH - 1, 1))
            around = above + below
            around = around + far + near
            around = around + up + down
            start = (c + 1) * COLS + base
            momentum = acc[start : start + 32, :]
            value = f + viscosity * (around - 6.0 * f) + coupling * (momentum - volume * f)
            fluid_next[c, ix] = value
            high, low = split2(value)
            halves[c * COLS + base : c * COLS + base + 32, :] = high
            halves[(3 + c) * COLS + base : (3 + c) * COLS + base + 32, :] = low
    store = pltpu.make_async_copy(fluid_next, next_h, store_sem)
    store.start()

    def sample(first, count):
        hots, cols = [], []
        for n in range(count):
            tile = blocks[first + n]
            cell = tile[1:2].astype(jnp.int32) - 1
            col, level = cell >> 9, cell & (DEPTH - 1)
            hots.append(jnp.where(z_sub == level, 1.0, 0.0).astype(BF16))
            cols.append(col_iota == col)
        along = jnp.dot(
            halves[...], jnp.concatenate(hots, axis=1), preferred_element_type=F32
        )
        for n in range(count):
            for c in range(3):
                part = along[:, n * BLK : (n + 1) * BLK]
                both = part[c * COLS : (c + 1) * COLS] + part[(3 + c) * COLS : (4 + c) * COLS]
                value = jnp.sum(jnp.where(cols[n], both, 0.0), axis=0, keepdims=True)
                sampled[first + n, c : c + 1, :] = value

    in_chunks(sample)
    for n in range(CAP):
        sampled[total + n] = blank
    for d in range(CODES):
        for k in range(CAP):
            base = d * BACK_ROWS + 3 * k
            answers[base : base + 3, :] = sampled[offset[d] + k, 0:3, :]
        answers[d * BACK_ROWS + 3 * CAP : (d + 1) * BACK_ROWS, :] = jnp.zeros(
            (BACK_ROWS - 3 * CAP, BLK), F32
        )
    store.wait()


def advance(early, late, fluid, xlo, xhi, ylo, yhi):
    sds = jax.ShapeDtypeStruct
    room = CODES * CAP + CAP + SMALL
    return pl.pallas_call(
        fluid_kernel,
        out_shape=(sds((3, 4, 32, DEPTH), F32), sds((CODES * BACK_ROWS, BLK), F32)),
        in_specs=[VMEM, VMEM, HBM] + [VMEM] * 4,
        out_specs=(HBM, VMEM),
        scratch_shapes=[
            pltpu.VMEM((3, 4, 32, DEPTH), F32),
            pltpu.VMEM((3, 4, 32, DEPTH), F32),
            pltpu.VMEM((room, 8, BLK), F32),
            pltpu.VMEM((room, 8, BLK), F32),
            pltpu.VMEM((4 * COLS, DEPTH), F32),
            pltpu.VMEM((6 * COLS, DEPTH), BF16),
            pltpu.SemaphoreType.DMA,
            pltpu.SemaphoreType.DMA,
        ],
        compiler_params=params(48),
    )(early, late, fluid, xlo, xhi, ylo, yhi)


def on_device(
    positions, velocities, radii, cell_of, block_route, ghost_list, tile_home, tile_partner, fluid
):
    pos = jnp.transpose(positions, (1, 0, 2))
    vel = jnp.transpose(velocities, (1, 0, 2))
    route = jnp.transpose(block_route, (1, 0))
    updated, slots, early, late, xlo, xhi, ylo, yhi = particles(
        tile_home, tile_partner, pos, vel, radii, cell_of, route, ghost_list, fluid
    )
    fluid_next, answers = advance(early, late, fluid, xlo, xhi, ylo, yhi)
    velocity_next = return_answers(slots, updated, answers)
    return jnp.transpose(velocity_next, (1, 0, 2)), fluid_next


def solution(mesh):
    placed = (
        P(("slab", "brick"), None, None),
        P(("slab", "brick"), None, None),
        P(("slab", "brick"), None),
        P(("slab", "brick"), None),
        P(("slab", "brick"), None),
        P(("slab", "brick")),
        P(("slab", "brick")),
        P(("slab", "brick")),
        P(None, "slab", "brick", None),
    )
    return jax.shard_map(
        on_device,
        mesh=mesh,
        in_specs=placed,
        out_specs=(P(("slab", "brick"), None, None), P(None, "slab", "brick", None)),
        check_vma=False,
    )
```

time: 109 us -> 75.8 us (0.70)
  Pallas kernels: 103 us -> 69 us
    pallas_call x1, Pallas kernels: 39.2 us -> 22.9 us  [return_answers(): pl.pallas_call(return_kernel, out_shape=jax.ShapeDtypeStruct((3, NB, BLK)...]
    pallas_call x1, Pallas kernels: 25.3 us -> 14 us  [advance(): pl.pallas_call(fluid_kernel, out_shape=(sds((3, 4, 32, DEPTH), F32), sds(...]
    pallas_call x3 -> x1, Pallas kernels: 38.3 us -> 32.1 us  [particles(): pl.pallas_call(particle_kernel, out_shape=(sds((3, NB, BLK), F32), sds((8...]
    unnamed x27 -> x21, local copies, waits for them, and re-layouts: 5 us -> 5.75 us
where the time goes in v2:
time: 75.8 us; the launch traced here: 75.4 us
  Pallas kernels  69 us (91%)
  local copies, waits for them, and re-layouts  5.75 us (8%)
    pallas_call x1, Pallas kernels, particles(): pl.pallas_call(particle_kernel, out_shape=(sds((3, NB, BLK), F32), sds((8...  32.1 us
    pallas_call x1, Pallas kernels, return_answers(): pl.pallas_call(return_kernel, out_shape=jax.ShapeDtypeStruct((3, NB, BLK)...  22.9 us
    pallas_call x1, Pallas kernels, advance(): pl.pallas_call(fluid_kernel, out_shape=(sds((3, 4, 32, DEPTH), F32), sds(...  14 us
    unnamed x21, local copies, waits for them, and re-layouts  5.75 us

profile of v2, /device:TPU:1, one launch (start us, length us, event | category | flops | bytes accessed | tf_op | source)
XLA Modules:
  0.0 75.4 jit_solution(18233942224834348722)
XLA Ops:
  0.6 0.0 copy-start.9
  0.6 0.0 copy-start.6
  0.7 0.0 copy-start.7
  0.7 0.0 copy-start.8
  0.7 0.6 copy-done.9
  1.3 0.0 copy-done.6
  1.3 0.0 copy-done.7
  1.3 0.0 copy-done.8
  1.3 0.0 copy-start
  1.3 1.1 %copy-done = f32[3,4,32,512]{3,2,1,0:T(8,128)S(1)} copy-done((f32[3,4,32,512]{3,2,1,0:T(8,128)S(1)}, f32[3,4,32,512]{3,2,1,0:T(8,128)}, u32[]{:S(2)}) %copy-start) | copy-done | bytes 786456
  2.5 0.0 copy-start.2
  2.5 0.9 %copy-done.2 = f32[64,3,128]{2,0,1:T(8,128)S(1)} copy-done((f32[64,3,128]{2,0,1:T(8,128)S(1)}, f32[64,3,128]{2,0,1:T(8,128)}, u32[]{:S(2)}) %copy-start.2) | copy-done | bytes 98328
  3.4 0.0 copy-start.3
  3.4 0.9 %copy-done.3 = f32[64,3,128]{2,0,1:T(8,128)S(1)} copy-done((f32[64,3,128]{2,0,1:T(8,128)S(1)}, f32[64,3,128]{2,0,1:T(8,128)}, u32[]{:S(2)}) %copy-start.3) | copy-done | bytes 98328
  4.3 0.0 copy-start.4
  4.3 0.8 %copy-done.4 = f32[64,128]{1,0:T(8,128)S(1)} copy-done((f32[64,128]{1,0:T(8,128)S(1)}, f32[64,128]{1,0:T(8,128)}, u32[]{:S(2)}) %copy-start.4) | copy-done | bytes 32792
  5.0 0.0 copy-start.5
  5.0 0.8 %copy-done.5 = s32[64,128]{1,0:T(8,128)S(1)} copy-done((s32[64,128]{1,0:T(8,128)S(1)}, s32[64,128]{1,0:T(8,128)}, u32[]{:S(2)}) %copy-start.5) | copy-done | bytes 32792
  5.8 0.0 copy-start.1
  5.8 32.1 %shard_map.104 = (f32[3,64,128]{2,1,0:T(8,128)S(1)}, s32[8,128]{1,0:T(8,128)S(1)}, f32[384,128]{1,0:T(8,128)S(1)}, f32[576,128]{1,0:T(8,128)S(1)}, f32[3,32,512]...) custom-call(s32[16]{0:T(128)S(1)} %copy-done.7, s32[128]{0:T(128)S(1)} %copy-done.6, ...), custom_call_target="tpu_custom_call" | custom-call | tf_op jit(solution)/shard_map/pallas_call | solution.py:306
  37.9 0.0 copy-done.1
  37.9 14.0 %shard_map.105 = (f32[3,4,32,512]{3,2,1,0:T(8,128)}, f32[576,128]{1,0:T(8,128)S(1)}) custom-call(f32[384,128]{1,0:T(8,128)S(1)} %get-tuple-element.14.early, f32[576,128]{1,0:T(8,128)S(1)} %get-tuple-element.15.late, f32[3,4,32,512]{3,2,1,0:T(8,128)S(1)} %copy-done.1, f32[3,32,512]{2,1,0:T(8,128)S(1)} %get-tuple-element.16.xlo, ...), custom_call_target="tpu_custom_call" | custom-call | tf_op jit(solution)/shard_map/pallas_call | solution.py:574
  51.9 22.9 %shard_map.106 = f32[3,64,128]{2,1,0:T(8,128)S(1)} custom-call(s32[8,128]{1,0:T(8,128)S(1)} %get-tuple-element.12.slots, f32[3,64,128]{2,1,0:T(8,128)S(1)} %get-tuple-element.13.updated, f32[576,128]{1,0:T(8,128)S(1)} %get-tuple-element.20.src), custom_call_target="tpu_custom_call" | custom-call | tf_op jit(solution)/shard_map/pallas_call | solution.py:413
  74.8 0.6 copy.12
Async XLA Ops:
  0.6 0.7 copy-start.9
  0.6 0.7 copy-start.6
  0.7 0.7 copy-start.7
  0.7 0.7 copy-start.8
  1.3 1.1 %copy-start = (f32[3,4,32,512]{3,2,1,0:T(8,128)S(1)}, f32[3,4,32,512]{3,2,1,0:T(8,128)}, u32[]{:S(2)}) copy-start(f32[3,4,32,512]{3,2,1,0:T(8,128)} %fluid_h.3) | copy-start | bytes 2359300
  2.5 0.9 %copy-start.2 = (f32[64,3,128]{2,0,1:T(8,128)S(1)}, f32[64,3,128]{2,0,1:T(8,128)}, u32[]{:S(2)}) copy-start(f32[64,3,128]{2,0,1:T(8,128)} %param.9) | copy-start | bytes 294916
  3.4 0.9 %copy-start.3 = (f32[64,3,128]{2,0,1:T(8,128)S(1)}, f32[64,3,128]{2,0,1:T(8,128)}, u32[]{:S(2)}) copy-start(f32[64,3,128]{2,0,1:T(8,128)} %param.10) | copy-start | bytes 294916
  4.3 0.8 %copy-start.4 = (f32[64,128]{1,0:T(8,128)S(1)}, f32[64,128]{1,0:T(8,128)}, u32[]{:S(2)}) copy-start(f32[64,128]{1,0:T(8,128)} %rad_h.1) | copy-start | bytes 98308
  5.0 0.8 %copy-start.5 = (s32[64,128]{1,0:T(8,128)S(1)}, s32[64,128]{1,0:T(8,128)}, u32[]{:S(2)}) copy-start(s32[64,128]{1,0:T(8,128)} %cell_h.1) | copy-start | bytes 98308
  5.8 32.1 %copy-start.1 = (f32[3,4,32,512]{3,2,1,0:T(8,128)S(1)}, f32[3,4,32,512]{3,2,1,0:T(8,128)}, u32[]{:S(2)}) copy-start(f32[3,4,32,512]{3,2,1,0:T(8,128)} %fluid_h.3) | copy-start | bytes 2359300

commit v3 on v2

--- a/solution.py
+++ b/solution.py
@@ -28,9 +28,10 @@
 CAND = 96
 CODES = 24
 CAP = 6
-EARLY_ROWS = 16
-LATE_ROWS = 24
-BACK_ROWS = 24
+EARLY_ROWS = 12
+LATE_ROWS = 18
+BACK_ROWS = 18
+ORDER = (4, 3, 5, 2, 6, 1, 7, 0)
 COLS = 128
 DEPTH = 512
 BIG = 16
@@ -66,24 +67,27 @@
     glist_h,
     home_h,
     partner_h,
-    home_v,
+    home_row_h,
     pos_h,
     vel_h,
     rad_h,
     cell_h,
     route_h,
     fluid_h,
-    updated,
-    slots,
+    updated_h,
+    slots_h,
     early,
     late,
     xlo,
     xhi,
     ylo,
     yhi,
+    updated,
+    slots,
     glist,
     home,
     partner,
+    home_row,
     pos,
     vel,
     rad,
@@ -109,6 +113,7 @@
     late_send,
     late_recv,
     local_sem,
+    store_sem,
 ):
     s, b = lax.axis_index("slab"), lax.axis_index("brick")
     upper_s = (lax.rem(s + 1, N_SLAB), b)
@@ -125,6 +130,7 @@
         (home_h, home),
         (partner_h, partner),
         (fluid_h, fluid),
+        (home_row_h, home_row),
     )
     loads = [pltpu.make_async_copy(a, z, load_sem.at[n]) for n, (a, z) in enumerate(pairs)]
     for load in loads:
@@ -176,9 +182,11 @@
     before = jnp.sum(jnp.where(earlier, 1.0, 0.0), axis=0, keepdims=True)
     slot = (code * CAP + before).astype(jnp.int32)
     slots[...] = jnp.broadcast_to(slot, (8, BLK))
+    keep_slots = pltpu.make_async_copy(slots, slots_h, store_sem.at[0])
+    keep_slots.start()
     upper_half = jnp.where(iota((1, BLK), 1) >= NB, 1, 0)
 
-    def lay_out(channels, rows, out, per):
+    def lay_out(channels, rows, out):
         groups = (len(channels) + 1) // 2
         for c, part in enumerate(channels):
             high, middle, low = split3(part)
@@ -191,22 +199,23 @@
         key = [slot * 8 + 2 * g + upper_half for g in range(groups)]
         key = jnp.concatenate(key, axis=1) if groups > 1 else key[0]
 
+        padded = (rows + 7) // 8 * 8
+
         def piece(part, _):
-            rho = iota((per, groups * BLK), 0) + part * per
-            q = rho % rows
-            want = ((rho // rows) * CAP + q // count) * 8 + q % count
-            want = jnp.where(q < count * CAP, want, -1)
+            rho = iota((8 * padded, groups * BLK), 0)
+            q = rho % padded
+            want = ((part * 8 + rho // padded) * CAP + q // count) * 8 + q % count
+            want = jnp.where(q < rows, want, -1)
             hot = jnp.where(want == key, 1.0, 0.0).astype(BF16)
             got = jnp.dot(hot, payload[0 : groups * BLK, :], preferred_element_type=F32)
-            out[pl.ds(pl.multiple_of(part * per, 8), per), :] = (
-                got[:, 0:BLK] + got[:, BLK : 2 * BLK] + got[:, 2 * BLK : 3 * BLK]
-            )
+            got = got[:, 0:BLK] + got[:, BLK : 2 * BLK] + got[:, 2 * BLK : 3 * BLK]
+            out[pl.ds(part * 8, 8)] = got.reshape(8, padded, BLK)[:, 0:rows, :]
             return 0
 
-        lax.fori_loop(0, CODES * rows // per, piece, 0)
-
-    lay_out([rad[...], cell[...].astype(F32) + 1.0], EARLY_ROWS, out_early, 192)
-    first = send_all(out_early, early, early_send, early_recv, local_sem.at[0], EARLY_ROWS, 1)
+        lax.fori_loop(0, CODES // 8, piece, 0)
+
+    lay_out([rad[...], cell[...].astype(F32) + 1.0], EARLY_ROWS, out_early)
+    first = send_all(out_early, early, early_send, early_recv, local_sem.at[0], 1)
     for copy in first:
         copy.start()
 
@@ -257,7 +266,7 @@
     for n in range(4):
         cand[NB + 8 * n : NB + 8 * (n + 1)] = ghosts[n].reshape(8, 8, BLK)
     lax.fori_loop(NB // 8, CAND // 8, features_of, 0)
-    for load in loads[6:8]:
+    for load in loads[6:8] + loads[9:]:
         load.wait()
 
     def tile_sum(t):
@@ -277,7 +286,7 @@
 
     lax.fori_loop(0, TILES // 8, tiles, 0)
 
-    belongs = jnp.where(iota((NB, TILES), 0) == home_v[...], 1.0, 0.0).astype(BF16)
+    belongs = jnp.where(iota((NB, TILES), 0) == home_row[...], 1.0, 0.0).astype(BF16)
 
     def gathered(c):
         pieces = jnp.concatenate(split3(terms[:, c, :]), axis=1)
@@ -293,11 +302,13 @@
         value = vel[c] + (a * weight_sum - gathered(c)) / mass
         updated[c] = value
         values.append(value)
-    lay_out(values, LATE_ROWS, out_late, 192)
-    second = send_all(out_late, late, late_send, late_recv, local_sem.at[1], LATE_ROWS, 1)
+    keep_updated = pltpu.make_async_copy(updated, updated_h, store_sem.at[1])
+    keep_updated.start()
+    lay_out(values, LATE_ROWS, out_late)
+    second = send_all(out_late, late, late_send, late_recv, local_sem.at[1], 1)
     for copy in second:
         copy.start()
-    for copy in halos[4:] + first + second:
+    for copy in halos[4:] + first + second + [keep_slots, keep_updated]:
         copy.wait()
 
 
@@ -308,19 +319,22 @@
         out_shape=(
             sds((3, NB, BLK), F32),
             sds((8, BLK), jnp.int32),
-            sds((CODES * EARLY_ROWS, BLK), F32),
-            sds((CODES * LATE_ROWS, BLK), F32),
+            sds((CODES, EARLY_ROWS, BLK), F32),
+            sds((CODES, LATE_ROWS, BLK), F32),
             sds((3, 32, DEPTH), F32),
             sds((3, 32, DEPTH), F32),
             sds((16, DEPTH), F32),
             sds((16, DEPTH), F32),
         ),
-        in_specs=[HBM] * 3 + [VMEM] + [HBM] * 6,
-        out_specs=(VMEM,) * 8,
+        in_specs=[HBM] * 10,
+        out_specs=(HBM,) * 8,
         scratch_shapes=[
+            pltpu.VMEM((3, NB, BLK), F32),
+            pltpu.VMEM((8, BLK), jnp.int32),
             pltpu.SMEM((16,), jnp.int32),
             pltpu.SMEM((TILES,), jnp.int32),
             pltpu.SMEM((TILES,), jnp.int32),
+            pltpu.VMEM((1, TILES), jnp.int32),
             pltpu.VMEM((3, NB, BLK), F32),
             pltpu.VMEM((3, NB, BLK), F32),
             pltpu.VMEM((NB, BLK), F32),
@@ -336,9 +350,9 @@
             pltpu.VMEM((CAND, 32, 2 * BLK), BF16),
             pltpu.VMEM((TILES, 8, BLK), F32),
             pltpu.VMEM((4 * NB, 3 * BLK), BF16),
-            pltpu.VMEM((CODES * EARLY_ROWS, BLK), F32),
-            pltpu.VMEM((CODES * LATE_ROWS, BLK), F32),
-            pltpu.SemaphoreType.DMA((9,)),
+            pltpu.VMEM((CODES, EARLY_ROWS, BLK), F32),
+            pltpu.VMEM((CODES, LATE_ROWS, BLK), F32),
+            pltpu.SemaphoreType.DMA((10,)),
             pltpu.SemaphoreType.DMA((8,)),
             pltpu.SemaphoreType.DMA((8,)),
             pltpu.SemaphoreType.DMA((CODES,)),
@@ -346,25 +360,22 @@
             pltpu.SemaphoreType.DMA((CODES,)),
             pltpu.SemaphoreType.DMA((CODES,)),
             pltpu.SemaphoreType.DMA((2,)),
+            pltpu.SemaphoreType.DMA((2,)),
         ],
-        compiler_params=params(40, 0),
+        compiler_params=params(56, 0),
     )(glist, home, partner, home.reshape(1, TILES), pos, vel, rad, cell, route, fluid)
 
 
-def send_all(src, dst, send_sem, recv_sem, local_sem, rows, sign):
+def send_all(src, dst, send_sem, recv_sem, local_sem, sign):
     s, b = lax.axis_index("slab"), lax.axis_index("brick")
-
-    def region(index):
-        return pl.ds(pl.multiple_of(index * rows, 8), rows)
-
     copies = []
-    for turn in range(N_BRICK):
+    for turn in ORDER:
         brick = lax.rem(b + turn, N_BRICK)
         for o in range(3):
             slab = lax.rem(s + N_SLAB + sign * (o - 1), N_SLAB)
             n = turn * 3 + o
-            source = src.at[region(o * N_BRICK + brick)]
-            target = dst.at[region(o * N_BRICK + b)]
+            source = src.at[o * N_BRICK + brick]
+            target = dst.at[o * N_BRICK + b]
             if turn == 0 and o == 1:
                 copies.append(pltpu.make_async_copy(source, target, local_sem))
             else:
@@ -391,21 +402,29 @@
             pl.semaphore_signal(barrier, inc=1, device_id=peer, device_id_type=MESH)
 
 
-def return_kernel(slots, updated, src, out, back, send_sem, recv_sem, local_sem):
+def return_kernel(
+    slots_h, updated_h, src, out, slots, updated, back, load_sem, send_sem, recv_sem, local_sem
+):
+    loads = [
+        pltpu.make_async_copy(slots_h.at[0], slots, load_sem.at[0]),
+        pltpu.make_async_copy(updated_h, updated, load_sem.at[1]),
+    ]
+    for load in loads:
+        load.start()
     barrier = pltpu.get_barrier_semaphore()
     greet_all(barrier)
     pl.semaphore_wait(barrier, 3 * N_BRICK - 1)
-    copies = send_all(src, back, send_sem, recv_sem, local_sem, BACK_ROWS, -1)
+    copies = send_all(src, back, send_sem, recv_sem, local_sem, -1)
     for copy in copies:
         copy.start()
-    for copy in copies:
+    for copy in loads + copies:
         copy.wait()
     for n in range(NB):
-        slot = slots[0, n]
-        first = (slot // CAP) * BACK_ROWS + (slot % CAP) * 3
+        slot = slots[n]
+        code, first = slot // CAP, (slot % CAP) * 3
         for c in range(3):
             here = updated[c, n : n + 1, :]
-            picked = back[pl.ds(first + c, 1), :]
+            picked = back[code, pl.ds(first + c, 1), :]
             out[c, n : n + 1, :] = here + relaxation * (picked - here)
 
 
@@ -413,29 +432,39 @@
     return pl.pallas_call(
         return_kernel,
         out_shape=jax.ShapeDtypeStruct((3, NB, BLK), F32),
-        in_specs=[SMEM, VMEM, VMEM],
+        in_specs=[HBM] * 3,
         out_specs=VMEM,
         scratch_shapes=[
-            pltpu.VMEM((CODES * BACK_ROWS, BLK), F32),
+            pltpu.SMEM((BLK,), jnp.int32),
+            pltpu.VMEM((3, NB, BLK), F32),
+            pltpu.VMEM((CODES, BACK_ROWS, BLK), F32),
+            pltpu.SemaphoreType.DMA((2,)),
             pltpu.SemaphoreType.DMA((CODES,)),
             pltpu.SemaphoreType.DMA((CODES,)),
             pltpu.SemaphoreType.DMA,
         ],
-        compiler_params=params(32, 1),
+        compiler_params=params(56, 1),
     )(slots, updated, answers)
 
 
 def fluid_kernel(
+    early_h,
+    late_h,
+    fluid_h,
+    xlo_h,
+    xhi_h,
+    ylo_h,
+    yhi_h,
+    next_h,
+    answers_h,
     early,
     late,
-    fluid_h,
+    fluid,
     xlo,
     xhi,
     ylo,
     yhi,
-    next_h,
     answers,
-    fluid,
     fluid_next,
     blocks,
     sampled,
@@ -444,11 +473,24 @@
     load_sem,
     store_sem,
 ):
-    load = pltpu.make_async_copy(fluid_h, fluid, load_sem)
-    load.start()
+    pairs = (
+        (early_h, early),
+        (late_h, late),
+        (fluid_h, fluid),
+        (xlo_h, xlo),
+        (xhi_h, xhi),
+        (ylo_h, ylo),
+        (yhi_h, yhi),
+    )
+    loads = [pltpu.make_async_copy(a, z, load_sem.at[n]) for n, (a, z) in enumerate(pairs)]
+    for load in loads:
+        load.start()
+    acc[...] = jnp.zeros_like(acc)
+    for load in loads[:2]:
+        load.wait()
     valid = jnp.zeros((CODES, 1), F32)
     for k in range(CAP):
-        cells = early[pl.ds(2 * k + 1, CODES, stride=EARLY_ROWS), :]
+        cells = early[:, 2 * k + 1, :]
         valid = valid + jnp.where(cells[:, 0:1] > 0.5, 1.0, 0.0)
     counted = valid.astype(jnp.int32)
     offset = []
@@ -456,14 +498,11 @@
     for d in range(CODES):
         offset.append(total)
         total = total + counted[d, 0]
-    acc[...] = jnp.zeros_like(acc)
     blank = jnp.zeros((8, BLK), F32)
     for d in range(CODES):
         for k in range(CAP):
-            base = d * EARLY_ROWS + 2 * k
-            blocks[offset[d] + k, 0:2, :] = early[base : base + 2, :]
-            base = d * LATE_ROWS + 3 * k
-            blocks[offset[d] + k, 2:5, :] = late[base : base + 3, :]
+            blocks[offset[d] + k, 0:2, :] = early[d, 2 * k : 2 * k + 2, :]
+            blocks[offset[d] + k, 2:5, :] = late[d, 3 * k : 3 * k + 3, :]
     for n in range(CAP):
         blocks[total + n] = blank
     big = total // BIG
@@ -506,7 +545,8 @@
         acc[...] += both[0 : 4 * COLS] + both[4 * COLS : 8 * COLS]
 
     in_chunks(deposit)
-    load.wait()
+    for load in loads[2:]:
+        load.wait()
 
     first_row = iota((32, DEPTH), 0) == 0
     last_row = iota((32, DEPTH), 0) == 31
@@ -560,12 +600,11 @@
         sampled[total + n] = blank
     for d in range(CODES):
         for k in range(CAP):
-            base = d * BACK_ROWS + 3 * k
-            answers[base : base + 3, :] = sampled[offset[d] + k, 0:3, :]
-        answers[d * BACK_ROWS + 3 * CAP : (d + 1) * BACK_ROWS, :] = jnp.zeros(
-            (BACK_ROWS - 3 * CAP, BLK), F32
-        )
+            answers[d, 3 * k : 3 * k + 3, :] = sampled[offset[d] + k, 0:3, :]
+    back = pltpu.make_async_copy(answers, answers_h, load_sem.at[0])
+    back.start()
     store.wait()
+    back.wait()
 
 
 def advance(early, late, fluid, xlo, xhi, ylo, yhi):
@@ -573,20 +612,27 @@
     room = CODES * CAP + CAP + SMALL
     return pl.pallas_call(
         fluid_kernel,
-        out_shape=(sds((3, 4, 32, DEPTH), F32), sds((CODES * BACK_ROWS, BLK), F32)),
-        in_specs=[VMEM, VMEM, HBM] + [VMEM] * 4,
-        out_specs=(HBM, VMEM),
+        out_shape=(sds((3, 4, 32, DEPTH), F32), sds((CODES, BACK_ROWS, BLK), F32)),
+        in_specs=[HBM] * 7,
+        out_specs=(HBM, HBM),
         scratch_shapes=[
+            pltpu.VMEM((CODES, EARLY_ROWS, BLK), F32),
+            pltpu.VMEM((CODES, LATE_ROWS, BLK), F32),
             pltpu.VMEM((3, 4, 32, DEPTH), F32),
+            pltpu.VMEM((3, 32, DEPTH), F32),
+            pltpu.VMEM((3, 32, DEPTH), F32),
+            pltpu.VMEM((16, DEPTH), F32),
+            pltpu.VMEM((16, DEPTH), F32),
+            pltpu.VMEM((CODES, BACK_ROWS, BLK), F32),
             pltpu.VMEM((3, 4, 32, DEPTH), F32),
             pltpu.VMEM((room, 8, BLK), F32),
             pltpu.VMEM((room, 8, BLK), F32),
             pltpu.VMEM((4 * COLS, DEPTH), F32),
             pltpu.VMEM((6 * COLS, DEPTH), BF16),
-            pltpu.SemaphoreType.DMA,
+            pltpu.SemaphoreType.DMA((7,)),
             pltpu.SemaphoreType.DMA,
         ],
-        compiler_params=params(48),
+        compiler_params=params(56),
     )(early, late, fluid, xlo, xhi, ylo, yhi)
 
 

time: 75.8 us -> 78.6 us (1.037)
  Pallas kernels: 69 us -> 76.2 us
  local copies, waits for them, and re-layouts: 5.75 us -> 1.54 us
    pallas_call x1, Pallas kernels: 22.9 us -> 28.2 us  [return_answers(): pl.pallas_call(return_kernel, out_shape=jax.ShapeDtypeStruct((3, NB, BLK)...]
    unnamed x21 -> x1, local copies, waits for them, and re-layouts: 5.75 us -> 1.54 us
    pallas_call x1, Pallas kernels: 14 us -> 17 us  [advance(): pl.pallas_call(fluid_kernel, out_shape=(sds((3, 4, 32, DEPTH), F32), sds(...]
    pallas_call x1, Pallas kernels: 32.1 us -> 31 us  [particles(): pl.pallas_call(particle_kernel, out_shape=(sds((3, NB, BLK), F32), sds((8...]
where the time goes in v3:
time: 78.6 us; the launch traced here: 78.4 us
  Pallas kernels  76.2 us (97%)
  local copies, waits for them, and re-layouts  1.54 us (2%)
    pallas_call x1, Pallas kernels, particles(): pl.pallas_call(particle_kernel, out_shape=(sds((3, NB, BLK), F32), sds((8...  31 us
    pallas_call x1, Pallas kernels, return_answers(): pl.pallas_call(return_kernel, out_shape=jax.ShapeDtypeStruct((3, NB, BLK)...  28.2 us
    pallas_call x1, Pallas kernels, advance(): pl.pallas_call(fluid_kernel, out_shape=(sds((3, 4, 32, DEPTH), F32), sds(...  17 us

profile of v3, /device:TPU:1, one launch (start us, length us, event | category | flops | bytes accessed | tf_op | source)
XLA Modules:
  0.0 78.4 jit_solution(11649302566991496459)
XLA Ops:
  0.6 31.0 %shard_map.104 = (f32[3,64,128]{2,1,0:T(8,128)}, s32[8,128]{1,0:T(8,128)}, f32[24,12,128]{2,1,0:T(8,128)}, f32[24,18,128]{2,1,0:T(8,128)}, f32[3,32,512]{2,1,0:T...) custom-call(s32[16]{0:T(128)} %glist_h.1, s32[128]{0:T(128)} %home_h.1, s32[128]{0:T(128)} %partner_h.1, ...), custom_call_target="tpu_custom_call" | custom-call | tf_op jit(solution)/shard_map/pallas_call | solution.py:317
  31.7 17.0 %shard_map.105 = (f32[3,4,32,512]{3,2,1,0:T(8,128)}, f32[24,18,128]{2,1,0:T(8,128)}) custom-call(f32[24,12,128]{2,1,0:T(8,128)} %get-tuple-element.14.early_h, f32[24,18,128]{2,1,0:T(8,128)} %get-tuple-element.15.late_h, f32[3,4,32,512]{3,2,1,0:T(8,128)} %fluid_h.3, f32[3,32,512]{2,1,0:T(8,128)} %get-tuple-element.16.xlo_h, ...), custom_call_target="tpu_custom_call" | custom-call | tf_op jit(solution)/shard_map/pallas_call | solution.py:613
  48.7 28.2 %shard_map.106 = f32[3,64,128]{2,1,0:T(8,128)} custom-call(s32[8,128]{1,0:T(8,128)} %get-tuple-element.12.slots_h, f32[3,64,128]{2,1,0:T(8,128)} %get-tuple-element.13.updated_h, f32[24,18,128]{2,1,0:T(8,128)} %get-tuple-element.20.src), custom_call_target="tpu_custom_call" | custom-call | tf_op jit(solution)/shard_map/pallas_call | solution.py:432
  76.9 1.5 %copy.12 = f32[64,3,128]{2,0,1:T(8,128)} copy(f32[64,3,128]{2,0,1:T(8,128)} %bitcast.5) | data formatting | bytes 196608

commit v4 on v3

--- a/solution.py
+++ b/solution.py
@@ -34,6 +34,7 @@
 ORDER = (4, 3, 5, 2, 6, 1, 7, 0)
 COLS = 128
 DEPTH = 512
+PER_STEP = 32
 BIG = 16
 SMALL = 4
 
@@ -57,7 +58,7 @@
 
 def params(mib, collective_id=None):
     return pltpu.CompilerParams(
-        vmem_limit_bytes=mib << 20,
+        vmem_limit_bytes=int(mib * 1024 * 1024),
         collective_id=collective_id,
         has_side_effects=collective_id is not None,
     )
@@ -78,6 +79,8 @@
     slots_h,
     early,
     late,
+    spread_h,
+    spread,
     xlo,
     xhi,
     ylo,
@@ -186,7 +189,7 @@
     keep_slots.start()
     upper_half = jnp.where(iota((1, BLK), 1) >= NB, 1, 0)
 
-    def lay_out(channels, rows, out):
+    def lay_out(channels, rows, out, copies):
         groups = (len(channels) + 1) // 2
         for c, part in enumerate(channels):
             high, middle, low = split3(part)
@@ -201,7 +204,7 @@
 
         padded = (rows + 7) // 8 * 8
 
-        def piece(part, _):
+        for part in range(3):
             rho = iota((8 * padded, groups * BLK), 0)
             q = rho % padded
             want = ((part * 8 + rho // padded) * CAP + q // count) * 8 + q % count
@@ -209,15 +212,13 @@
             hot = jnp.where(want == key, 1.0, 0.0).astype(BF16)
             got = jnp.dot(hot, payload[0 : groups * BLK, :], preferred_element_type=F32)
             got = got[:, 0:BLK] + got[:, BLK : 2 * BLK] + got[:, 2 * BLK : 3 * BLK]
-            out[pl.ds(part * 8, 8)] = got.reshape(8, padded, BLK)[:, 0:rows, :]
-            return 0
-
-        lax.fori_loop(0, CODES // 8, piece, 0)
-
-    lay_out([rad[...], cell[...].astype(F32) + 1.0], EARLY_ROWS, out_early)
+            out[part * 8 : part * 8 + 8] = got.reshape(8, padded, BLK)[:, 0:rows, :]
+        for turn in zip(*copies):
+            for copy in turn:
+                copy.start()
+
     first = send_all(out_early, early, early_send, early_recv, local_sem.at[0], 1)
-    for copy in first:
-        copy.start()
+    lay_out([rad[...], cell[...].astype(F32) + 1.0], EARLY_ROWS, out_early, first)
 
     loads[8].wait()
     for c in range(3):
@@ -280,11 +281,12 @@
         return out[0:8] + out[8:16] + out[16:24]
 
     def tiles(step, _):
-        for n, value in enumerate([tile_sum(step * 8 + n) for n in range(8)]):
-            terms[step * 8 + n] = value
+        first = step * PER_STEP
+        for n, value in enumerate([tile_sum(first + n) for n in range(PER_STEP)]):
+            terms[first + n] = value
         return 0
 
-    lax.fori_loop(0, TILES // 8, tiles, 0)
+    lax.fori_loop(0, TILES // PER_STEP, tiles, 0)
 
     belongs = jnp.where(iota((NB, TILES), 0) == home_row[...], 1.0, 0.0).astype(BF16)
 
@@ -304,11 +306,32 @@
         values.append(value)
     keep_updated = pltpu.make_async_copy(updated, updated_h, store_sem.at[1])
     keep_updated.start()
-    lay_out(values, LATE_ROWS, out_late)
     second = send_all(out_late, late, late_send, late_recv, local_sem.at[1], 1)
-    for copy in second:
-        copy.start()
-    for copy in halos[4:] + first + second + [keep_slots, keep_updated]:
+    lay_out(values, LATE_ROWS, out_late, second)
+
+    for copy in halos[4:]:
+        copy.wait()
+    first_row = iota((32, DEPTH), 0) == 0
+    last_row = iota((32, DEPTH), 0) == 31
+    first_z = iota((32, DEPTH), 1) == 0
+    last_z = iota((32, DEPTH), 1) == DEPTH - 1
+    for ix in range(4):
+        for c in range(3):
+            f = fluid[c, ix]
+            below = xlo[c] if ix == 0 else fluid[c, ix - 1]
+            above = xhi[c] if ix == 3 else fluid[c, ix + 1]
+            at = c * 4 + ix
+            near = jnp.where(first_row, ylo[at : at + 1, :], pltpu.roll(f, 1, 0))
+            far = jnp.where(last_row, yhi[at : at + 1, :], pltpu.roll(f, 31, 0))
+            down = jnp.where(first_z, 0.0, pltpu.roll(f, 1, 1))
+            up = jnp.where(last_z, 0.0, pltpu.roll(f, DEPTH - 1, 1))
+            around = above + below
+            around = around + far + near
+            around = around + up + down
+            spread[c, ix] = f + viscosity * (around - 6.0 * f)
+    keep_spread = pltpu.make_async_copy(spread, spread_h, store_sem.at[2])
+    keep_spread.start()
+    for copy in sum(first + second, []) + [keep_slots, keep_updated, keep_spread]:
         copy.wait()
 
 
@@ -321,14 +344,16 @@
             sds((8, BLK), jnp.int32),
             sds((CODES, EARLY_ROWS, BLK), F32),
             sds((CODES, LATE_ROWS, BLK), F32),
-            sds((3, 32, DEPTH), F32),
-            sds((3, 32, DEPTH), F32),
-            sds((16, DEPTH), F32),
-            sds((16, DEPTH), F32),
+            sds((3, 4, 32, DEPTH), F32),
         ),
         in_specs=[HBM] * 10,
-        out_specs=(HBM,) * 8,
+        out_specs=(HBM,) * 5,
         scratch_shapes=[
+            pltpu.VMEM((3, 4, 32, DEPTH), F32),
+            pltpu.VMEM((3, 32, DEPTH), F32),
+            pltpu.VMEM((3, 32, DEPTH), F32),
+            pltpu.VMEM((16, DEPTH), F32),
+            pltpu.VMEM((16, DEPTH), F32),
             pltpu.VMEM((3, NB, BLK), F32),
             pltpu.VMEM((8, BLK), jnp.int32),
             pltpu.SMEM((16,), jnp.int32),
@@ -360,7 +385,7 @@
             pltpu.SemaphoreType.DMA((CODES,)),
             pltpu.SemaphoreType.DMA((CODES,)),
             pltpu.SemaphoreType.DMA((2,)),
-            pltpu.SemaphoreType.DMA((2,)),
+            pltpu.SemaphoreType.DMA((3,)),
         ],
         compiler_params=params(56, 0),
     )(glist, home, partner, home.reshape(1, TILES), pos, vel, rad, cell, route, fluid)
@@ -368,7 +393,7 @@
 
 def send_all(src, dst, send_sem, recv_sem, local_sem, sign):
     s, b = lax.axis_index("slab"), lax.axis_index("brick")
-    copies = []
+    copies = [[], [], []]
     for turn in ORDER:
         brick = lax.rem(b + turn, N_BRICK)
         for o in range(3):
@@ -377,9 +402,9 @@
             source = src.at[o * N_BRICK + brick]
             target = dst.at[o * N_BRICK + b]
             if turn == 0 and o == 1:
-                copies.append(pltpu.make_async_copy(source, target, local_sem))
+                copies[o].append(pltpu.make_async_copy(source, target, local_sem))
             else:
-                copies.append(
+                copies[o].append(
                     pltpu.make_async_remote_copy(
                         src_ref=source,
                         dst_ref=target,
@@ -414,7 +439,8 @@
     barrier = pltpu.get_barrier_semaphore()
     greet_all(barrier)
     pl.semaphore_wait(barrier, 3 * N_BRICK - 1)
-    copies = send_all(src, back, send_sem, recv_sem, local_sem, -1)
+    by_offset = send_all(src, back, send_sem, recv_sem, local_sem, -1)
+    copies = [copy for turn in zip(*by_offset) for copy in turn]
     for copy in copies:
         copy.start()
     for copy in loads + copies:
@@ -443,7 +469,7 @@
             pltpu.SemaphoreType.DMA((CODES,)),
             pltpu.SemaphoreType.DMA,
         ],
-        compiler_params=params(56, 1),
+        compiler_params=params(53.5, 1),
     )(slots, updated, answers)
 
 
@@ -451,19 +477,13 @@
     early_h,
     late_h,
     fluid_h,
-    xlo_h,
-    xhi_h,
-    ylo_h,
-    yhi_h,
+    spread_h,
     next_h,
     answers_h,
     early,
     late,
     fluid,
-    xlo,
-    xhi,
-    ylo,
-    yhi,
+    spread,
     answers,
     fluid_next,
     blocks,
@@ -477,10 +497,7 @@
         (early_h, early),
         (late_h, late),
         (fluid_h, fluid),
-        (xlo_h, xlo),
-        (xhi_h, xhi),
-        (ylo_h, ylo),
-        (yhi_h, yhi),
+        (spread_h, spread),
     )
     loads = [pltpu.make_async_copy(a, z, load_sem.at[n]) for n, (a, z) in enumerate(pairs)]
     for load in loads:
@@ -548,28 +565,14 @@
     for load in loads[2:]:
         load.wait()
 
-    first_row = iota((32, DEPTH), 0) == 0
-    last_row = iota((32, DEPTH), 0) == 31
-    first_z = iota((32, DEPTH), 1) == 0
-    last_z = iota((32, DEPTH), 1) == DEPTH - 1
     for ix in range(4):
         base = ix * 32
         volume = acc[base : base + 32, :]
         for c in range(3):
             f = fluid[c, ix]
-            below = xlo[c] if ix == 0 else fluid[c, ix - 1]
-            above = xhi[c] if ix == 3 else fluid[c, ix + 1]
-            row = c * 4 + ix
-            near = jnp.where(first_row, ylo[row : row + 1, :], pltpu.roll(f, 1, 0))
-            far = jnp.where(last_row, yhi[row : row + 1, :], pltpu.roll(f, 31, 0))
-            down = jnp.where(first_z, 0.0, pltpu.roll(f, 1, 1))
-            up = jnp.where(last_z, 0.0, pltpu.roll(f, DEPTH - 1, 1))
-            around = above + below
-            around = around + far + near
-            around = around + up + down
             start = (c + 1) * COLS + base
             momentum = acc[start : start + 32, :]
-            value = f + viscosity * (around - 6.0 * f) + coupling * (momentum - volume * f)
+            value = spread[c, ix] + coupling * (momentum - volume * f)
             fluid_next[c, ix] = value
             high, low = split2(value)
             halves[c * COLS + base : c * COLS + base + 32, :] = high
@@ -607,33 +610,30 @@
     back.wait()
 
 
-def advance(early, late, fluid, xlo, xhi, ylo, yhi):
+def advance(early, late, fluid, spread):
     sds = jax.ShapeDtypeStruct
     room = CODES * CAP + CAP + SMALL
     return pl.pallas_call(
         fluid_kernel,
         out_shape=(sds((3, 4, 32, DEPTH), F32), sds((CODES, BACK_ROWS, BLK), F32)),
-        in_specs=[HBM] * 7,
+        in_specs=[HBM] * 4,
         out_specs=(HBM, HBM),
         scratch_shapes=[
             pltpu.VMEM((CODES, EARLY_ROWS, BLK), F32),
             pltpu.VMEM((CODES, LATE_ROWS, BLK), F32),
             pltpu.VMEM((3, 4, 32, DEPTH), F32),
-            pltpu.VMEM((3, 32, DEPTH), F32),
-            pltpu.VMEM((3, 32, DEPTH), F32),
-            pltpu.VMEM((16, DEPTH), F32),
-            pltpu.VMEM((16, DEPTH), F32),
+            pltpu.VMEM((3, 4, 32, DEPTH), F32),
             pltpu.VMEM((CODES, BACK_ROWS, BLK), F32),
             pltpu.VMEM((3, 4, 32, DEPTH), F32),
             pltpu.VMEM((room, 8, BLK), F32),
             pltpu.VMEM((room, 8, BLK), F32),
             pltpu.VMEM((4 * COLS, DEPTH), F32),
             pltpu.VMEM((6 * COLS, DEPTH), BF16),
-            pltpu.SemaphoreType.DMA((7,)),
+            pltpu.SemaphoreType.DMA((4,)),
             pltpu.SemaphoreType.DMA,
         ],
         compiler_params=params(56),
-    )(early, late, fluid, xlo, xhi, ylo, yhi)
+    )(early, late, fluid, spread)
 
 
 def on_device(
@@ -642,10 +642,10 @@
     pos = jnp.transpose(positions, (1, 0, 2))
     vel = jnp.transpose(velocities, (1, 0, 2))
     route = jnp.transpose(block_route, (1, 0))
-    updated, slots, early, late, xlo, xhi, ylo, yhi = particles(
+    updated, slots, early, late, spread = particles(
         tile_home, tile_partner, pos, vel, radii, cell_of, route, ghost_list, fluid
     )
-    fluid_next, answers = advance(early, late, fluid, xlo, xhi, ylo, yhi)
+    fluid_next, answers = advance(early, late, fluid, spread)
     velocity_next = return_answers(slots, updated, answers)
     return jnp.transpose(velocity_next, (1, 0, 2)), fluid_next
 

time: 78.6 us -> 67.6 us (0.86)
  Pallas kernels: 76.2 us -> 66.2 us
  local copies, waits for them, and re-layouts: 1.54 us -> 0.65 us
    pallas_call x1, Pallas kernels: 28.2 us -> 19.3 us  [return_answers(): pl.pallas_call(return_kernel, out_shape=jax.ShapeDtypeStruct((3, NB, BLK)...]
    pallas_call x1, Pallas kernels: 31 us -> 27.3 us  [particles(): pl.pallas_call(particle_kernel, out_shape=(sds((3, NB, BLK), F32), sds((8...]
    pallas_call x1, Pallas kernels: 17 us -> 19.6 us  [advance(): pl.pallas_call(fluid_kernel, out_shape=(sds((3, 4, 32, DEPTH), F32), sds(...]
    unnamed x1 -> x5, local copies, waits for them, and re-layouts: 1.54 us -> 0.65 us
where the time goes in v4:
time: 67.6 us; the launch traced here: 67.5 us
  Pallas kernels  66.2 us (98%)
  between operations  0.69 us (1%)
    pallas_call x1, Pallas kernels, particles(): pl.pallas_call(particle_kernel, out_shape=(sds((3, NB, BLK), F32), sds((8...  27.3 us
    pallas_call x1, Pallas kernels, advance(): pl.pallas_call(fluid_kernel, out_shape=(sds((3, 4, 32, DEPTH), F32), sds(...  19.6 us
    pallas_call x1, Pallas kernels, return_answers(): pl.pallas_call(return_kernel, out_shape=jax.ShapeDtypeStruct((3, NB, BLK)...  19.3 us

profile of v4, /device:TPU:1, one launch (start us, length us, event | category | flops | bytes accessed | tf_op | source)
XLA Modules:
  0.0 67.5 jit_solution(12897130593094434668)
XLA Ops:
  0.6 27.3 %shard_map.104 = (f32[3,64,128]{2,1,0:T(8,128)}, s32[8,128]{1,0:T(8,128)}, f32[24,12,128]{2,1,0:T(8,128)}, f32[24,18,128]{2,1,0:T(8,128)}, f32[3,4,32,512]{3,2,1,0:T(8,128)}) custom-call(s32[16]{0:T(128)} %glist_h.1, s32[128]{0:T(128)} %home_h.1, s32[128]{0:T(128)} %partner_h.1, s32[1,128]{1,0:T(1,128)} %bitcast.8, f32[3,64,128]{2,1,0:T(8,128)} %bitcast.6, ...), custom_call_target="tpu_custom_call" | custom-call | tf_op jit(solution)/shard_map/pallas_call | solution.py:340
  28.0 0.0 copy-start
  28.0 0.0 copy-start.1
  28.0 19.6 %shard_map.105 = (f32[3,4,32,512]{3,2,1,0:T(8,128)}, f32[24,18,128]{2,1,0:T(8,128)}) custom-call(f32[24,12,128]{2,1,0:T(8,128)} %get-tuple-element.11.early_h, f32[24,18,128]{2,1,0:T(8,128)} %get-tuple-element.12.late_h, f32[3,4,32,512]{3,2,1,0:T(8,128)} %fluid_h.3, f32[3,4,32,512]{3,2,1,0:T(8,128)} %get-tuple-element.13.spread_h), custom_call_target="tpu_custom_call" | custom-call | tf_op jit(solution)/shard_map/pallas_call | solution.py:616
  47.6 0.0 copy-done
  47.6 0.0 copy-done.1
  47.6 19.3 %shard_map.106 = f32[3,64,128]{2,1,0:T(8,128)S(1)} custom-call(s32[8,128]{1,0:T(8,128)S(1)} %copy-done.1, f32[3,64,128]{2,1,0:T(8,128)S(1)} %copy-done, f32[24,18,128]{2,1,0:T(8,128)} %get-tuple-element.14.src), custom_call_target="tpu_custom_call" | custom-call | tf_op jit(solution)/shard_map/pallas_call | solution.py:458
  66.9 0.6 copy.12
Async XLA Ops:
  28.0 19.6 %copy-start = (f32[3,64,128]{2,1,0:T(8,128)S(1)}, f32[3,64,128]{2,1,0:T(8,128)}, u32[]{:S(2)}) copy-start(f32[3,64,128]{2,1,0:T(8,128)} %get-tuple-element.10.updated_h) | copy-start | bytes 294916
  28.0 19.6 %copy-start.1 = (s32[8,128]{1,0:T(8,128)S(1)}, s32[8,128]{1,0:T(8,128)}, u32[]{:S(2)}) copy-start(s32[8,128]{1,0:T(8,128)} %get-tuple-element.9.slots_h) | copy-start | bytes 12292

commit v5 on v4

--- a/solution.py
+++ b/solution.py
@@ -34,8 +34,9 @@
 ORDER = (4, 3, 5, 2, 6, 1, 7, 0)
 COLS = 128
 DEPTH = 512
-PER_STEP = 32
+PER_STEP = 64
 BIG = 16
+MIDDLE = 8
 SMALL = 4
 
 
@@ -204,7 +205,7 @@
 
         padded = (rows + 7) // 8 * 8
 
-        for part in range(3):
+        for part in (0, 2, 1):
             rho = iota((8 * padded, groups * BLK), 0)
             q = rho % padded
             want = ((part * 8 + rho // padded) * CAP + q // count) * 8 + q % count
@@ -213,8 +214,7 @@
             got = jnp.dot(hot, payload[0 : groups * BLK, :], preferred_element_type=F32)
             got = got[:, 0:BLK] + got[:, BLK : 2 * BLK] + got[:, 2 * BLK : 3 * BLK]
             out[part * 8 : part * 8 + 8] = got.reshape(8, padded, BLK)[:, 0:rows, :]
-        for turn in zip(*copies):
-            for copy in turn:
+            for copy in copies[part]:
                 copy.start()
 
     first = send_all(out_early, early, early_send, early_recv, local_sem.at[0], 1)
@@ -486,16 +486,15 @@
     spread,
     answers,
     fluid_next,
-    blocks,
-    sampled,
+    order,
     acc,
     halves,
     load_sem,
     store_sem,
 ):
     pairs = (
-        (early_h, early),
-        (late_h, late),
+        (early_h, early.at[pl.ds(0, CODES)]),
+        (late_h, late.at[pl.ds(0, CODES)]),
         (fluid_h, fluid),
         (spread_h, spread),
     )
@@ -507,7 +506,7 @@
         load.wait()
     valid = jnp.zeros((CODES, 1), F32)
     for k in range(CAP):
-        cells = early[:, 2 * k + 1, :]
+        cells = early[0:CODES, 2 * k + 1, :]
         valid = valid + jnp.where(cells[:, 0:1] > 0.5, 1.0, 0.0)
     counted = valid.astype(jnp.int32)
     offset = []
@@ -515,27 +514,38 @@
     for d in range(CODES):
         offset.append(total)
         total = total + counted[d, 0]
-    blank = jnp.zeros((8, BLK), F32)
     for d in range(CODES):
         for k in range(CAP):
-            blocks[offset[d] + k, 0:2, :] = early[d, 2 * k : 2 * k + 2, :]
-            blocks[offset[d] + k, 2:5, :] = late[d, 3 * k : 3 * k + 3, :]
-    for n in range(CAP):
-        blocks[total + n] = blank
+            order[offset[d] + k] = d * 8 + k
+    for n in range(SMALL):
+        order[total + n] = CODES * 8
+    early[CODES] = jnp.zeros((EARLY_ROWS, BLK), F32)
+    late[CODES] = jnp.zeros((LATE_ROWS, BLK), F32)
     big = total // BIG
-    small = (total - big * BIG + SMALL - 1) // SMALL
+    left_over = total - big * BIG
+    middle = (left_over + SMALL - 1) // MIDDLE
+    left_over = jnp.maximum(left_over - middle * MIDDLE, 0)
+    small = (left_over + SMALL - 1) // SMALL
 
     def in_chunks(run):
-        def big_step(step, _):
-            run(step * BIG, BIG)
-            return 0
-
-        def small_step(step, _):
-            run(big * BIG + step * SMALL, SMALL)
-            return 0
-
-        lax.fori_loop(0, big, big_step, 0)
-        lax.fori_loop(0, small, small_step, 0)
+        def steps(count, first, size):
+            def step(n, _):
+                run(first + n * size, size)
+                return 0
+
+            lax.fori_loop(0, count, step, 0)
+
+        steps(big, 0, BIG)
+        steps(middle, big * BIG, MIDDLE)
+        steps(small, big * BIG + middle * MIDDLE, SMALL)
+
+    def place(n):
+        at = order[n]
+        return at >> 3, at & 7
+
+    def cells_of(d, k):
+        cell = early[d, pl.ds(2 * k + 1, 1), :].astype(jnp.int32) - 1
+        return cell >> 9, cell & (DEPTH - 1)
 
     col_iota = iota((COLS, BLK), 0)
     z_sub = iota((DEPTH, BLK), 0)
@@ -544,13 +554,12 @@
     def deposit(first, count):
         left, right = [[], []], []
         for n in range(count):
-            tile = blocks[first + n]
-            cell = tile[1:2].astype(jnp.int32) - 1
-            col, level = cell >> 9, cell & (DEPTH - 1)
-            radius = tile[0:1]
+            d, k = place(first + n)
+            col, level = cells_of(d, k)
+            radius = early[d, pl.ds(2 * k, 1), :]
             mass = radius * radius * radius
             hot = jnp.where(col_iota == col, 1.0, 0.0).astype(BF16)
-            pieces = [split2(x) for x in [mass] + [mass * tile[2 + c : 3 + c] for c in range(3)]]
+            pieces = [split2(x) for x in [mass] + [mass * late[d, pl.ds(3 * k + c, 1), :] for c in range(3)]]
             for which in range(2):
                 left[which].append(jnp.concatenate([hot * p[which] for p in pieces], axis=0))
             depth_tile = jnp.broadcast_to(level.astype(F32), (BLK, BLK))
@@ -583,28 +592,22 @@
     def sample(first, count):
         hots, cols = [], []
         for n in range(count):
-            tile = blocks[first + n]
-            cell = tile[1:2].astype(jnp.int32) - 1
-            col, level = cell >> 9, cell & (DEPTH - 1)
+            col, level = cells_of(*place(first + n))
             hots.append(jnp.where(z_sub == level, 1.0, 0.0).astype(BF16))
             cols.append(col_iota == col)
         along = jnp.dot(
             halves[...], jnp.concatenate(hots, axis=1), preferred_element_type=F32
         )
         for n in range(count):
+            d, k = place(first + n)
             for c in range(3):
                 part = along[:, n * BLK : (n + 1) * BLK]
                 both = part[c * COLS : (c + 1) * COLS] + part[(3 + c) * COLS : (4 + c) * COLS]
                 value = jnp.sum(jnp.where(cols[n], both, 0.0), axis=0, keepdims=True)
-                sampled[first + n, c : c + 1, :] = value
+                answers[d, pl.ds(3 * k + c, 1), :] = value
 
     in_chunks(sample)
-    for n in range(CAP):
-        sampled[total + n] = blank
-    for d in range(CODES):
-        for k in range(CAP):
-            answers[d, 3 * k : 3 * k + 3, :] = sampled[offset[d] + k, 0:3, :]
-    back = pltpu.make_async_copy(answers, answers_h, load_sem.at[0])
+    back = pltpu.make_async_copy(answers.at[pl.ds(0, CODES)], answers_h, load_sem.at[0])
     back.start()
     store.wait()
     back.wait()
@@ -619,14 +622,13 @@
         in_specs=[HBM] * 4,
         out_specs=(HBM, HBM),
         scratch_shapes=[
-            pltpu.VMEM((CODES, EARLY_ROWS, BLK), F32),
-            pltpu.VMEM((CODES, LATE_ROWS, BLK), F32),
+            pltpu.VMEM((CODES + 1, EARLY_ROWS, BLK), F32),
+            pltpu.VMEM((CODES + 1, LATE_ROWS, BLK), F32),
             pltpu.VMEM((3, 4, 32, DEPTH), F32),
             pltpu.VMEM((3, 4, 32, DEPTH), F32),
-            pltpu.VMEM((CODES, BACK_ROWS, BLK), F32),
+            pltpu.VMEM((CODES + 1, BACK_ROWS, BLK), F32),
             pltpu.VMEM((3, 4, 32, DEPTH), F32),
-            pltpu.VMEM((room, 8, BLK), F32),
-            pltpu.VMEM((room, 8, BLK), F32),
+            pltpu.SMEM((room,), jnp.int32),
             pltpu.VMEM((4 * COLS, DEPTH), F32),
             pltpu.VMEM((6 * COLS, DEPTH), BF16),
             pltpu.SemaphoreType.DMA((4,)),

time: 67.6 us -> 64.5 us (0.954)
  Pallas kernels: 66.2 us -> 63.1 us
    pallas_call x1, Pallas kernels: 19.3 us -> 12.8 us  [return_answers(): pl.pallas_call(return_kernel, out_shape=jax.ShapeDtypeStruct((3, NB, BLK)...]
    pallas_call x1, Pallas kernels: 19.6 us -> 24.2 us  [advance(): pl.pallas_call(fluid_kernel, out_shape=(sds((3, 4, 32, DEPTH), F32), sds(...]
    pallas_call x1, Pallas kernels: 27.3 us -> 26 us  [particles(): pl.pallas_call(particle_kernel, out_shape=(sds((3, NB, BLK), F32), sds((8...]
where the time goes in v5:
time: 64.5 us; the launch traced here: 64.4 us
  Pallas kernels  63.1 us (98%)
  between operations  0.69 us (1%)
  local copies, waits for them, and re-layouts  0.65 us (1%)
    pallas_call x1, Pallas kernels, particles(): pl.pallas_call(particle_kernel, out_shape=(sds((3, NB, BLK), F32), sds((8...  26 us
    pallas_call x1, Pallas kernels, advance(): pl.pallas_call(fluid_kernel, out_shape=(sds((3, 4, 32, DEPTH), F32), sds(...  24.2 us
    pallas_call x1, Pallas kernels, return_answers(): pl.pallas_call(return_kernel, out_shape=jax.ShapeDtypeStruct((3, NB, BLK)...  12.8 us

profile of v5, /device:TPU:1, one launch (start us, length us, event | category | flops | bytes accessed | tf_op | source)
XLA Modules:
  0.0 64.4 jit_solution(4247319324807496322)
XLA Ops:
  0.6 26.0 %shard_map.104 = (f32[3,64,128]{2,1,0:T(8,128)}, s32[8,128]{1,0:T(8,128)}, f32[24,12,128]{2,1,0:T(8,128)}, f32[24,18,128]{2,1,0:T(8,128)}, f32[3,4,32,512]{3,2,1,0:T(8,128)}) custom-call(s32[16]{0:T(128)} %glist_h.1, s32[128]{0:T(128)} %home_h.1, s32[128]{0:T(128)} %partner_h.1, s32[1,128]{1,0:T(1,128)} %bitcast.8, f32[3,64,128]{2,1,0:T(8,128)} %bitcast.6, ...), custom_call_target="tpu_custom_call" | custom-call | tf_op jit(solution)/shard_map/pallas_call | solution.py:340
  26.7 0.0 copy-start
  26.7 0.0 copy-start.1
  26.7 24.2 %shard_map.105 = (f32[3,4,32,512]{3,2,1,0:T(8,128)}, f32[24,18,128]{2,1,0:T(8,128)}) custom-call(f32[24,12,128]{2,1,0:T(8,128)} %get-tuple-element.11.early_h, f32[24,18,128]{2,1,0:T(8,128)} %get-tuple-element.12.late_h, f32[3,4,32,512]{3,2,1,0:T(8,128)} %fluid_h.3, f32[3,4,32,512]{3,2,1,0:T(8,128)} %get-tuple-element.13.spread_h), custom_call_target="tpu_custom_call" | custom-call | tf_op jit(solution)/shard_map/pallas_call | solution.py:619
  50.9 0.0 copy-done
  50.9 0.0 copy-done.1
  50.9 12.8 %shard_map.106 = f32[3,64,128]{2,1,0:T(8,128)S(1)} custom-call(s32[8,128]{1,0:T(8,128)S(1)} %copy-done.1, f32[3,64,128]{2,1,0:T(8,128)S(1)} %copy-done, f32[24,18,128]{2,1,0:T(8,128)} %get-tuple-element.14.src), custom_call_target="tpu_custom_call" | custom-call | tf_op jit(solution)/shard_map/pallas_call | solution.py:458
  63.7 0.6 copy.12
Async XLA Ops:
  26.7 24.2 %copy-start = (f32[3,64,128]{2,1,0:T(8,128)S(1)}, f32[3,64,128]{2,1,0:T(8,128)}, u32[]{:S(2)}) copy-start(f32[3,64,128]{2,1,0:T(8,128)} %get-tuple-element.10.updated_h) | copy-start | bytes 294916
  26.7 24.2 %copy-start.1 = (s32[8,128]{1,0:T(8,128)S(1)}, s32[8,128]{1,0:T(8,128)}, u32[]{:S(2)}) copy-start(s32[8,128]{1,0:T(8,128)} %get-tuple-element.9.slots_h) | copy-start | bytes 12292

commit v6 on v5

--- a/solution.py
+++ b/solution.py
@@ -35,8 +35,7 @@
 COLS = 128
 DEPTH = 512
 PER_STEP = 64
-BIG = 16
-MIDDLE = 8
+CHUNKS = (32, 16, 8, 4)
 SMALL = 4
 
 
@@ -521,23 +520,22 @@
         order[total + n] = CODES * 8
     early[CODES] = jnp.zeros((EARLY_ROWS, BLK), F32)
     late[CODES] = jnp.zeros((LATE_ROWS, BLK), F32)
-    big = total // BIG
-    left_over = total - big * BIG
-    middle = (left_over + SMALL - 1) // MIDDLE
-    left_over = jnp.maximum(left_over - middle * MIDDLE, 0)
-    small = (left_over + SMALL - 1) // SMALL
+    counts = [total // CHUNKS[0]]
+    left_over = total - counts[0] * CHUNKS[0]
+    for size in CHUNKS[1:]:
+        counts.append((left_over + SMALL - 1) // size)
+        left_over = jnp.maximum(left_over - counts[-1] * size, 0)
 
     def in_chunks(run):
-        def steps(count, first, size):
+        first = 0
+        for count, size in zip(counts, CHUNKS):
+
             def step(n, _):
                 run(first + n * size, size)
                 return 0
 
             lax.fori_loop(0, count, step, 0)
-
-        steps(big, 0, BIG)
-        steps(middle, big * BIG, MIDDLE)
-        steps(small, big * BIG + middle * MIDDLE, SMALL)
+            first = first + count * size
 
     def place(n):
         at = order[n]

time: 64.5 us -> 63 us (0.977)
  Pallas kernels: 63.1 us -> 61.6 us
    pallas_call x1, Pallas kernels: 24.2 us -> 16.3 us  [advance(): pl.pallas_call(fluid_kernel, out_shape=(sds((3, 4, 32, DEPTH), F32), sds(...]
    pallas_call x1, Pallas kernels: 12.8 us -> 19.3 us  [return_answers(): pl.pallas_call(return_kernel, out_shape=jax.ShapeDtypeStruct((3, NB, BLK)...]
where the time goes in v6:
time: 63 us; the launch traced here: 62.9 us
  Pallas kernels  61.6 us (98%)
  between operations  0.69 us (1%)
  local copies, waits for them, and re-layouts  0.65 us (1%)
    pallas_call x1, Pallas kernels, particles(): pl.pallas_call(particle_kernel, out_shape=(sds((3, NB, BLK), F32), sds((8...  26 us
    pallas_call x1, Pallas kernels, return_answers(): pl.pallas_call(return_kernel, out_shape=jax.ShapeDtypeStruct((3, NB, BLK)...  19.3 us
    pallas_call x1, Pallas kernels, advance(): pl.pallas_call(fluid_kernel, out_shape=(sds((3, 4, 32, DEPTH), F32), sds(...  16.3 us

profile of v6, /device:TPU:1, one launch (start us, length us, event | category | flops | bytes accessed | tf_op | source)
XLA Modules:
  0.0 62.9 jit_solution(8347310951294333971)
XLA Ops:
  0.6 26.0 %shard_map.104 = (f32[3,64,128]{2,1,0:T(8,128)}, s32[8,128]{1,0:T(8,128)}, f32[24,12,128]{2,1,0:T(8,128)}, f32[24,18,128]{2,1,0:T(8,128)}, f32[3,4,32,512]{3,2,1,0:T(8,128)}) custom-call(s32[16]{0:T(128)} %glist_h.1, s32[128]{0:T(128)} %home_h.1, s32[128]{0:T(128)} %partner_h.1, s32[1,128]{1,0:T(1,128)} %bitcast.8, f32[3,64,128]{2,1,0:T(8,128)} %bitcast.6, ...), custom_call_target="tpu_custom_call" | custom-call | tf_op jit(solution)/shard_map/pallas_call | solution.py:339
  26.7 0.0 copy-start
  26.7 0.0 copy-start.1
  26.7 16.3 %shard_map.105 = (f32[3,4,32,512]{3,2,1,0:T(8,128)}, f32[24,18,128]{2,1,0:T(8,128)}) custom-call(f32[24,12,128]{2,1,0:T(8,128)} %get-tuple-element.11.early_h, f32[24,18,128]{2,1,0:T(8,128)} %get-tuple-element.12.late_h, f32[3,4,32,512]{3,2,1,0:T(8,128)} %fluid_h.3, f32[3,4,32,512]{3,2,1,0:T(8,128)} %get-tuple-element.13.spread_h), custom_call_target="tpu_custom_call" | custom-call | tf_op jit(solution)/shard_map/pallas_call | solution.py:617
  43.0 0.0 copy-done
  43.0 0.0 copy-done.1
  43.0 19.3 %shard_map.106 = f32[3,64,128]{2,1,0:T(8,128)S(1)} custom-call(s32[8,128]{1,0:T(8,128)S(1)} %copy-done.1, f32[3,64,128]{2,1,0:T(8,128)S(1)} %copy-done, f32[24,18,128]{2,1,0:T(8,128)} %get-tuple-element.14.src), custom_call_target="tpu_custom_call" | custom-call | tf_op jit(solution)/shard_map/pallas_call | solution.py:457
  62.3 0.6 %copy.12 = f32[64,3,128]{2,0,1:T(8,128)} copy(f32[64,3,128]{2,0,1:T(8,128)S(1)} %bitcast.5) | data formatting | bytes 196608
Async XLA Ops:
  26.7 16.3 %copy-start = (f32[3,64,128]{2,1,0:T(8,128)S(1)}, f32[3,64,128]{2,1,0:T(8,128)}, u32[]{:S(2)}) copy-start(f32[3,64,128]{2,1,0:T(8,128)} %get-tuple-element.10.updated_h) | copy-start | bytes 294916
  26.7 16.3 %copy-start.1 = (s32[8,128]{1,0:T(8,128)S(1)}, s32[8,128]{1,0:T(8,128)}, u32[]{:S(2)}) copy-start(s32[8,128]{1,0:T(8,128)} %get-tuple-element.9.slots_h) | copy-start | bytes 12292

commit v7 on v6

--- a/solution.py
+++ b/solution.py
@@ -34,8 +34,8 @@
 ORDER = (4, 3, 5, 2, 6, 1, 7, 0)
 COLS = 128
 DEPTH = 512
-PER_STEP = 64
-CHUNKS = (32, 16, 8, 4)
+PER_STEP = 128
+CHUNKS = (48, 16, 8, 4)
 SMALL = 4
 
 

time: 63 us -> 67.2 us (1.067); the launches traced: 62.9 us -> 66.4 us
  Pallas kernels: 61.6 us -> 65 us
    pallas_call x1, Pallas kernels: 19.3 us -> 21.8 us  [return_answers(): pl.pallas_call(return_kernel, out_shape=jax.ShapeDtypeStruct((3, NB, BLK)...]
    pallas_call x1, Pallas kernels: 16.3 us -> 18.3 us  [advance(): pl.pallas_call(fluid_kernel, out_shape=(sds((3, 4, 32, DEPTH), F32), sds(...]
    pallas_call x1, Pallas kernels: 26 us -> 25 us  [particles(): pl.pallas_call(particle_kernel, out_shape=(sds((3, NB, BLK), F32), sds((8...]
where the time goes in v7:
time: 67.2 us; the launch traced here: 66.4 us
  Pallas kernels  65 us (97%)
  between operations  0.69 us (1%)
    pallas_call x1, Pallas kernels, particles(): pl.pallas_call(particle_kernel, out_shape=(sds((3, NB, BLK), F32), sds((8...  25 us
    pallas_call x1, Pallas kernels, return_answers(): pl.pallas_call(return_kernel, out_shape=jax.ShapeDtypeStruct((3, NB, BLK)...  21.8 us
    pallas_call x1, Pallas kernels, advance(): pl.pallas_call(fluid_kernel, out_shape=(sds((3, 4, 32, DEPTH), F32), sds(...  18.3 us

profile of v7, /device:TPU:1, one launch (start us, length us, event | category | flops | bytes accessed | tf_op | source)
XLA Modules:
  0.0 66.4 jit_solution(10322251442471521430)
XLA Ops:
  0.6 25.0 %shard_map.104 = (f32[3,64,128]{2,1,0:T(8,128)}, s32[8,128]{1,0:T(8,128)}, f32[24,12,128]{2,1,0:T(8,128)}, f32[24,18,128]{2,1,0:T(8,128)}, f32[3,4,32,512]{3,2,1,0:T(8,128)}) custom-call(s32[16]{0:T(128)} %glist_h.1, s32[128]{0:T(128)} %home_h.1, s32[128]{0:T(128)} %partner_h.1, s32[1,128]{1,0:T(1,128)} %bitcast.8, f32[3,64,128]{2,1,0:T(8,128)} %bitcast.6, ...), custom_call_target="tpu_custom_call" | custom-call | tf_op jit(solution)/shard_map/pallas_call | solution.py:339
  25.6 0.0 copy-start
  25.6 0.0 copy-start.1
  25.6 18.3 %shard_map.105 = (f32[3,4,32,512]{3,2,1,0:T(8,128)}, f32[24,18,128]{2,1,0:T(8,128)}) custom-call(f32[24,12,128]{2,1,0:T(8,128)} %get-tuple-element.11.early_h, f32[24,18,128]{2,1,0:T(8,128)} %get-tuple-element.12.late_h, f32[3,4,32,512]{3,2,1,0:T(8,128)} %fluid_h.3, f32[3,4,32,512]{3,2,1,0:T(8,128)} %get-tuple-element.13.spread_h), custom_call_target="tpu_custom_call" | custom-call | tf_op jit(solution)/shard_map/pallas_call | solution.py:617
  43.9 0.0 copy-done
  43.9 0.0 copy-done.1
  43.9 21.8 %shard_map.106 = f32[3,64,128]{2,1,0:T(8,128)S(1)} custom-call(s32[8,128]{1,0:T(8,128)S(1)} %copy-done.1, f32[3,64,128]{2,1,0:T(8,128)S(1)} %copy-done, f32[24,18,128]{2,1,0:T(8,128)} %get-tuple-element.14.src), custom_call_target="tpu_custom_call" | custom-call | tf_op jit(solution)/shard_map/pallas_call | solution.py:457
  65.7 0.6 copy.12
Async XLA Ops:
  25.6 18.3 %copy-start = (f32[3,64,128]{2,1,0:T(8,128)S(1)}, f32[3,64,128]{2,1,0:T(8,128)}, u32[]{:S(2)}) copy-start(f32[3,64,128]{2,1,0:T(8,128)} %get-tuple-element.10.updated_h) | copy-start | bytes 294916
  25.6 18.3 %copy-start.1 = (s32[8,128]{1,0:T(8,128)S(1)}, s32[8,128]{1,0:T(8,128)}, u32[]{:S(2)}) copy-start(s32[8,128]{1,0:T(8,128)} %get-tuple-element.9.slots_h) | copy-start | bytes 12292
